TPU v7x, 1024 devices: a whole 4x4x32 slice. The times are simulated.
1024 devices in a mesh: ta: 4 (over x), gx: 32 (over z), gy: 8 (over y, core).
Axes of the slice: x: 4, y: 4, z: 32, core: 2. Of those that a mesh axis runs over, the one named last changes fastest.
Arguments:
- eigvecs: bfloat16 [4, 32, 16, 24, 3, 2, 128], P('ta', 'gx', 'gy'), may hold values from -6 to 6
- links: bfloat16 [4, 32, 16, 24, 3, 2, 3, 3], P('ta', 'gx', 'gy'), may hold values from -4 to 4
- op_dirs: int32 [8], replicated, may hold values from 0 to 6, as said below
- op_moms: int32 [8], replicated, may hold values from 0 to 2
- perams: bfloat16 [128, 2, 512, 512], P(('ta', 'gx')), may hold values from -0.25 to 0.25
- pair_times: int32 [128, 2], P(('ta', 'gx')), may hold values from 0 to 3
- slot_counts: int32 [128], P(('ta', 'gx')), may hold values from 1 to 1, as said below
Outputs:
- margins: float32 [4, 8, 2, 128, 128], P('ta', 'gy')
- correlators: float32 [128, 8, 2], P(('ta', 'gx'), 'gy')
Inputs may be any that keep to these rules, and one draw needn't show every extreme that they name: Owner k holds slot k of the slot dimension; slot_counts[k] is 1 in every draw. `op_dirs`: codes 0, 1, 2 step forward along the first, second, third dimension, codes 3, 4, 5 step backward along them, code 6 is no displacement. Every code is used by some operator. `op_moms`: momentum in units of 2 pi / 24.
All inputs are finite; a program needn't handle non-finite values.
Results may differ from a plain program's by a relative error of at most 0.0061.
Values may be sent and summed in bfloat16 or wider, within the bound.
A program may use at most 32 MiB of HBM per device.

v0:
```python
import math

import jax
import jax.numpy as jnp
from jax import lax
from jax.sharding import PartitionSpec as P


def padded(block, sides, width):
    for axis, dim in sides:
        count = lax.axis_size(axis)
        forward = [(i, i + 1) for i in range(count - 1)]
        forward.append((count - 1, 0))
        backward = [(target, source) for source, target in forward]
        low = lax.ppermute(
            lax.slice_in_dim(block, block.shape[dim] - width, None, axis=dim), axis, forward
        )
        high = lax.ppermute(lax.slice_in_dim(block, 0, width, axis=dim), axis, backward)
        block = jnp.concatenate([low, block, high], axis=dim)
    return block


def color_apply(link_dir, vec_field):
    link_real = link_dir[..., 0, :, :]
    link_imag = link_dir[..., 1, :, :]
    field_real = vec_field[..., :, 0, :]
    field_imag = vec_field[..., :, 1, :]
    real_part = jnp.einsum(
        "...ab,...bn->...an", link_real, field_real, preferred_element_type=jnp.float32
    ) - jnp.einsum("...ab,...bn->...an", link_imag, field_imag, preferred_element_type=jnp.float32)
    imag_part = jnp.einsum(
        "...ab,...bn->...an", link_real, field_imag, preferred_element_type=jnp.float32
    ) + jnp.einsum("...ab,...bn->...an", link_imag, field_real, preferred_element_type=jnp.float32)
    return jnp.stack([real_part, imag_part], axis=-2)


def color_adjoint(link_dir, vec_field):
    link_real = link_dir[..., 0, :, :]
    link_imag = link_dir[..., 1, :, :]
    field_real = vec_field[..., :, 0, :]
    field_imag = vec_field[..., :, 1, :]
    real_part = jnp.einsum(
        "...ba,...bn->...an", link_real, field_real, preferred_element_type=jnp.float32
    ) + jnp.einsum("...ba,...bn->...an", link_imag, field_imag, preferred_element_type=jnp.float32)
    imag_part = jnp.einsum(
        "...ba,...bn->...an", link_real, field_imag, preferred_element_type=jnp.float32
    ) - jnp.einsum("...ba,...bn->...an", link_imag, field_real, preferred_element_type=jnp.float32)
    return jnp.stack([real_part, imag_part], axis=-2)


def phase_turn(values, momentum, z_coord):
    angle = 2.0 * math.pi * momentum.astype(jnp.float32) * z_coord / z_coord.shape[0]
    cosine = jnp.cos(angle)[:, None, None]
    sine = jnp.sin(angle)[:, None, None]
    values_real = values[..., 0, :]
    values_imag = values[..., 1, :]
    return jnp.stack(
        [cosine * values_real - sine * values_imag, sine * values_real + cosine * values_imag],
        axis=-2,
    )


def margin_block(left_matrix, displaced):
    vectors = displaced.shape[-1]
    rotated = jnp.stack([displaced[..., 1, :], -displaced[..., 0, :]], axis=-2)
    right_matrix = jnp.concatenate(
        [displaced.reshape(-1, vectors), rotated.reshape(-1, vectors)], axis=1
    )
    product = jnp.dot(left_matrix.T, right_matrix, preferred_element_type=jnp.float32)
    return product.reshape(vectors, 2, vectors).transpose(1, 0, 2)


def contract(tau_matrix, sink_margin, source_margin):
    order = tau_matrix.shape[-1]
    vectors = sink_margin.shape[-1]
    spins = order // vectors
    count_ops = sink_margin.shape[0]
    sink_real = sink_margin[:, 0]
    sink_imag = sink_margin[:, 1]
    source_real = source_margin[:, 0]
    source_imag = source_margin[:, 1]
    rows_real = tau_matrix[0].reshape(spins, vectors, order)
    rows_imag = tau_matrix[1].reshape(spins, vectors, order)
    left_real = jnp.einsum(
        "oab,sbc->osac", sink_real, rows_real, preferred_element_type=jnp.float32
    ) - jnp.einsum("oab,sbc->osac", sink_imag, rows_imag, preferred_element_type=jnp.float32)
    left_imag = jnp.einsum(
        "oab,sbc->osac", sink_real, rows_imag, preferred_element_type=jnp.float32
    ) + jnp.einsum("oab,sbc->osac", sink_imag, rows_real, preferred_element_type=jnp.float32)
    cols_real = tau_matrix[0].reshape(order, spins, vectors)
    cols_imag = tau_matrix[1].reshape(order, spins, vectors)
    right_real = jnp.einsum(
        "isd,ocd->oisc", cols_real, source_real, preferred_element_type=jnp.float32
    ) + jnp.einsum("isd,ocd->oisc", cols_imag, source_imag, preferred_element_type=jnp.float32)
    right_imag = jnp.einsum(
        "isd,ocd->oisc", cols_imag, source_real, preferred_element_type=jnp.float32
    ) - jnp.einsum("isd,ocd->oisc", cols_real, source_imag, preferred_element_type=jnp.float32)
    left_real = left_real.reshape(count_ops, order, order)
    left_imag = left_imag.reshape(count_ops, order, order)
    right_real = right_real.reshape(count_ops, order, order)
    right_imag = right_imag.reshape(count_ops, order, order)
    trace_real = jnp.sum(left_real * right_real + left_imag * right_imag, axis=(1, 2))
    trace_imag = jnp.sum(left_imag * right_real - left_real * right_imag, axis=(1, 2))
    return jnp.stack([trace_real, trace_imag], axis=-1) / vectors


def per_device(eigvecs, links, op_dirs, op_moms, perams, pair_times, slot_counts):
    eigen_field = eigvecs[0]
    link_field = links[0]
    cells_x = eigen_field.shape[0]
    cells_y = eigen_field.shape[1]
    cells_z = eigen_field.shape[2]
    vectors = eigen_field.shape[-1]
    carried = [
        color_adjoint(link_field[..., d, :, :, :], eigen_field).astype(jnp.bfloat16)
        for d in range(3)
    ]
    padded_first = padded(jnp.stack([eigen_field, carried[0]]), (("gx", 1),), 1)
    padded_second = padded(jnp.stack([eigen_field, carried[1]]), (("gy", 2),), 1)
    forward = [
        padded_first[0, 2 : cells_x + 2],
        padded_second[0, :, 2 : cells_y + 2],
        jnp.roll(eigen_field, -1, axis=2),
    ]
    behind = [
        padded_first[1, 0:cells_x],
        padded_second[1, :, 0:cells_y],
        jnp.roll(carried[2], 1, axis=2),
    ]
    shifted = [color_apply(link_field[..., d, :, :, :], forward[d]) for d in range(3)]
    shifted = (
        shifted
        + [piece.astype(jnp.float32) for piece in behind]
        + [eigen_field.astype(jnp.float32)]
    )
    stacked = jnp.stack(shifted)
    z_coord = jnp.arange(cells_z, dtype=jnp.float32)
    left_matrix = eigen_field.reshape(-1, vectors)
    norm_factor = 1.0 / math.sqrt(
        3.0 * cells_x * lax.axis_size("gx") * cells_y * lax.axis_size("gy") * cells_z
    )
    op_rows = []
    for o in range(op_dirs.shape[0]):
        chosen = lax.dynamic_index_in_dim(stacked, op_dirs[o], 0, keepdims=False)
        displaced = phase_turn(chosen, op_moms[o], z_coord).astype(jnp.bfloat16)
        op_rows.append(margin_block(left_matrix, displaced))
    partial_sums = jnp.stack(op_rows) * norm_factor
    ops_local = op_dirs.shape[0] // lax.axis_size("gy")
    summed = lax.psum(partial_sums, ("gx", "gy"))
    own_ops = lax.dynamic_slice_in_dim(summed, lax.axis_index("gy") * ops_local, ops_local, 0)
    margin_out = own_ops[None]
    every_time = lax.all_gather(own_ops.astype(jnp.bfloat16)[None], "ta", axis=0, tiled=True)
    live_count = slot_counts[0]
    tau_matrix = lax.dynamic_index_in_dim(perams, 0, 0, keepdims=False)
    pair_row = lax.dynamic_index_in_dim(pair_times, 0, 0, keepdims=False)
    sink_margin = lax.dynamic_index_in_dim(every_time, pair_row[0], 0, keepdims=False)
    source_margin = lax.dynamic_index_in_dim(every_time, pair_row[1], 0, keepdims=False)
    value_here = contract(tau_matrix, sink_margin, source_margin)
    results = [jnp.where(0 < live_count, value_here, jnp.zeros_like(value_here))]
    correlators = jnp.stack(results)
    return (margin_out, correlators)


def solution(mesh):
    placed = (
        P("ta", "gx", "gy", None, None, None, None),
        P("ta", "gx", "gy", None, None, None, None, None),
        P(),
        P(),
        P(("ta", "gx"), None, None, None),
        P(("ta", "gx"), None),
        P(("ta", "gx")),
    )
    return jax.shard_map(
        per_device,
        mesh=mesh,
        in_specs=placed,
        out_specs=(P("ta", "gy", None, None, None), P(("ta", "gx"), "gy", None)),
        check_vma=False,
    )
```

profile of v0, /device:TPU:24, one launch (start us, length us, event | category | flops | bytes accessed | tf_op | source)
XLA Modules:
  0.0 751.1 jit_solution(14698228453625599022)
XLA Ops:
  7.2 0.9 copy.283
  8.2 0.7 copy-done.5
  8.9 0.3 copy.277
  10.9 3.8 collective-permute-start.2
  14.8 16.8 %collective-permute-start = (bf16[2,1,2,24,3,2,128]{6,3,5,4,2,1,0:T(8,128)(2,1)S(1)}, bf16[2,1,2,24,3,2,128]{6,3,5,4,2,1,0:T(8,128)(2,1)S(1)}, u32[]{:S(2)}, u32[]{:S(2)}) collective-permute-start(bf16[2,1,2,24,3,2,128]{6,3,5,4,2,1,0:T(8,128)(2,1)S(1)} %get-tuple-element.54), channel_id=1, source_target_pairs={{8,0},{16,8},{24,16},{32,24},{40,32},{48,40},{56,48},{64,56},{72,6... | collective-permute-start | bytes 442376 | tf_op jit(solution)/shard_map/ppermute | solution.py:18
  31.6 1.7 collective-permute-start.1
  33.3 0.7 fusion.146
  44.3 0.3 fusion.96
  44.6 0.3 fusion.92
  45.5 0.2 fusion.93
  45.8 0.4 copy-done.4
  46.2 0.7 fusion.145
  57.3 0.2 fusion.56
  57.6 0.3 fusion.58
  57.8 0.3 fusion.60
  58.1 0.3 fusion.62
  58.7 0.3 fusion.66
  58.9 0.3 fusion.68
  59.2 0.3 fusion.70
  61.5 0.3 fusion.7
  61.9 0.3 fusion.11
  62.4 0.3 fusion.15
  62.8 0.3 fusion.19
  63.3 0.3 fusion.23
  63.7 0.3 fusion.27
  64.1 0.3 fusion.31
  64.6 0.3 fusion.35
  65.1 1.1 broadcast_multiply_fusion
  66.3 0.7 copy-done.6
  67.0 0.6 fusion.144
  72.4 641.8 %all-reduce.2.cloned.1.call-done = f32[8,2,128,128]{3,2,1,0:T(8,128)} async-done(((f32[8,2,128,128]{3,2,1,0:T(8,128)}), f32[8,2,128,128]{3,2,1,0:T(8,128)}) %all-reduce.2.cloned.1.call-update) | async-done | bytes 1048592 | tf_op jit(solution)/shard_map/psum | solution.py:149
  714.2 0.9 dynamic-slice_convert_fusion
  715.1 12.6 %all-gather = bf16[4,2,128,128]{3,2,1,0:T(8,128)(2,1)S(1)} all-gather(bf16[1,2,128,128]{3,2,1,0:T(8,128)(2,1)S(1)} %dynamic-slice_convert_fusion), channel_id=2, replica_groups=mesh['ta'=4,'gx'=32,'gy'=8] {'ta'}, dimensions={0}, use_global_device_ids=true | all-gather | bytes 327680 | tf_op jit(solution)/shard_map/all_gather | solution.py:152
  727.6 0.3 fusion.80
  727.9 0.3 fusion.81
  728.2 1.3 fusion
  729.5 2.5 reshape.1081
  732.0 2.5 copy.378
  734.6 1.3 fusion.2
  735.9 1.6 reshape.1080
  737.4 0.4 copy.377
  737.8 0.3 fusion.78
  738.1 0.3 fusion.79
  738.4 0.3 fusion.3
  738.7 0.9 copy-done.1
  739.6 1.2 add_reduce_fusion
  740.8 1.9 broadcast_select_fusion
  742.7 1.6 dynamic-slice_bitcast_fusion.8
  (134 shorter events, 7.1 us)
Async XLA Ops:
  7.2 1.0 copy-start
  7.2 707.0 %all-reduce.2.cloned.1.call-start = ((), (), s32[]{:S(2)}) async-start(), calls=%async_computation | async-start | bytes 2097152 | tf_op jit(solution)/shard_map/psum | solution.py:149
  8.1 0.7 copy-start.5
  10.9 48.6 %collective-permute-start.2 = (bf16[2,1,2,24,3,2,128]{6,3,5,4,2,1,0:T(8,128)(2,1)S(1)}, bf16[2,1,2,24,3,2,128]{6,3,5,4,2,1,0:T(8,128)(2,1)S(1)}, u32[]{:S(2)}, u32[]{:S(2)}) collective-permute-start(bf16[2,1,2,24,3,2,128]{6,3,5,4,2,1,0:T(8,128)(2,1)S(1)} %get-tuple-element.54), channel_id=1, source_target_pairs={{0,8},{8,16},{16,24},{24,32},{32,40},{40,48},{48,56},{56,64},{64,7... | collective-permute-start | bytes 442376 | tf_op jit(solution)/shard_map/ppermute | solution.py:15
  14.8 43.6 %collective-permute-start = (bf16[2,1,2,24,3,2,128]{6,3,5,4,2,1,0:T(8,128)(2,1)S(1)}, bf16[2,1,2,24,3,2,128]{6,3,5,4,2,1,0:T(8,128)(2,1)S(1)}, u32[]{:S(2)}, u32[]{:S(2)}) collective-permute-start(bf16[2,1,2,24,3,2,128]{6,3,5,4,2,1,0:T(8,128)(2,1)S(1)} %get-tuple-element.54), channel_id=1, source_target_pairs={{8,0},{16,8},{24,16},{32,24},{40,32},{48,40},{56,48},{64,56},{72,6... | collective-permute-start | bytes 442376 | tf_op jit(solution)/shard_map/ppermute | solution.py:18
  31.6 1.8 copy-start.3
  31.6 28.0 %collective-permute-start.3 = (bf16[2,1,1,24,3,2,128]{6,3,5,4,2,1,0:T(8,128)(2,1)S(1)}, bf16[2,1,1,24,3,2,128]{6,3,5,4,2,1,0:T(8,128)(2,1)S(1)}, u32[]{:S(2)}, u32[]{:S(2)}) collective-permute-start(bf16[2,1,1,24,3,2,128]{6,3,5,4,2,1,0:T(8,128)(2,1)S(1)} %get-tuple-element.33), channel_id=1, source_target_pairs={{0,1},{1,2},{2,3},{3,4},{4,5},{5,6},{6,7},{7,0},{8,9},{9,10},{10,1... | collective-permute-start | bytes 221192 | tf_op jit(solution)/shard_map/ppermute | solution.py:15
  31.6 25.7 %collective-permute-start.1 = (bf16[2,1,1,24,3,2,128]{6,3,5,4,2,1,0:T(8,128)(2,1)S(1)}, bf16[2,1,1,24,3,2,128]{6,3,5,4,2,1,0:T(8,128)(2,1)S(1)}, u32[]{:S(2)}, u32[]{:S(2)}) collective-permute-start(bf16[2,1,1,24,3,2,128]{6,3,5,4,2,1,0:T(8,128)(2,1)S(1)} %get-tuple-element.34), channel_id=1, source_target_pairs={{1,0},{2,1},{3,2},{4,3},{5,4},{6,5},{7,6},{0,7},{9,8},{10,9},{11,1... | collective-permute-start | bytes 221192 | tf_op jit(solution)/shard_map/ppermute | solution.py:18
  45.5 0.7 copy-start.4
  66.2 4.4 copy-start.2
  66.2 0.7 copy-start.6
  738.4 1.2 copy-start.1
Sparse Core Ops, SparseCore 0:
  66.4 647.7 all-reduce.1
where the time goes:
time: 753 us; the launch traced here: 751 us
  waiting for transfers between devices  642 us (85%)
  between operations  39.2 us (5%)
  starting transfers between devices  22.4 us (3%)
  local copies, waits for them, and re-layouts  18.1 us (2%)
  blocking collectives  12.6 us (2%)
  matrix products  12.4 us (2%)
    psum x1, waiting for transfers between devices, per_device(): summed = lax.psum(partial_sums, ('gx', 'gy'))  642 us
    ppermute x2, starting transfers between devices, padded(): lax.ppermute(lax.slice_in_dim(block, 0, width, axis=dim), axis, backward)  18.5 us
  transfers between devices with their start and end apart: 5, of which 1 were waited for; matrix products, arithmetic and copies ran while one was open for 1% of the time, Pallas kernels for 0%

commit v1 on v0

v1 whole, which is shorter than its diff:
```python
import math

import jax
import jax.numpy as jnp
from jax import lax
from jax.experimental import pallas as pl
from jax.experimental.pallas import tpu as pltpu
from jax.sharding import PartitionSpec as P

MESH = pl.DeviceIdType.MESH
DELTAS = (-1, 0, 1, 2)
F32 = jnp.float32
BF16 = jnp.bfloat16


def iota(shape, dim):
    return lax.broadcasted_iota(jnp.int32, shape, dim)


def ones_where(cond):
    return jnp.where(cond, 1.0, 0.0).astype(F32)


def mm(a, b):
    return jnp.dot(a, b, preferred_element_type=F32)


def mm_nt(a, b):
    return lax.dot_general(a, b, (((1,), (1,)), ((), ())), preferred_element_type=F32)


def peers(sizes):
    n_ta, n_gx, n_gy = sizes
    wanted = [(0, -1, 0), (0, 0, -1)]
    wanted += [(0, delta, j) for j in range(n_gy) for delta in DELTAS]
    wanted += [(0, step, 0) for step in (2, -2)]
    if n_gx > 8:
        wanted += [(0, step, 0) for step in (4, -4)]
    wanted += [(jt, delta, 0) for jt in range(n_ta) for delta in DELTAS]
    seen = []
    for ta, gx, gy in wanted:
        at = (ta % n_ta, gx % n_gx, gy % n_gy)
        if at != (0, 0, 0) and at not in seen:
            seen.append(at)
    return seen


def kernel(
    sizes, cells_z, norm_factor,
    dirs_ref, moms_ref, pair_ref, v_ref, links_ref, perams_ref,
    margin_ref, corr_ref,
    tau_ref, halo_x, halo_y, field, turned, left, cos_ref, sin_ref, part, recv, total, relay_r, relay_l, every,
    tau_sem, halo_send, halo_recv, part_send, part_recv, relay_send, relay_recv, last_send, last_recv,
):
    n_ta, n_gx, n_gy = sizes
    ta, gx, gy = (lax.axis_index(axis) for axis in ("ta", "gx", "gy"))
    layer = cells_z * 6
    cells_y = v_ref.shape[0] // layer
    n_relay = n_gx // 8

    def device(dta, dgx, dgy):
        return {
            "ta": lax.rem(ta + dta % n_ta, n_ta),
            "gx": lax.rem(gx + dgx % n_gx, n_gx),
            "gy": lax.rem(gy + dgy % n_gy, n_gy),
        }

    def remote(src, dst, send_sem, recv_sem, *offset):
        return pltpu.make_async_remote_copy(
            src_ref=src, dst_ref=dst, send_sem=send_sem, recv_sem=recv_sem,
            device_id=device(*offset), device_id_type=MESH,
        )

    barrier = pltpu.get_barrier_semaphore()
    known = peers(sizes)
    for dta, dgx, dgy in known:
        pl.semaphore_signal(
            barrier, inc=1, device_id=device(-dta, -dgx, -dgy), device_id_type=MESH
        )
    tau_copy = pltpu.make_async_copy(perams_ref, tau_ref, tau_sem)
    tau_copy.start()

    pl.semaphore_wait(barrier, len(known))
    send_x = remote(v_ref, halo_x, halo_send.at[0], halo_recv.at[0], 0, -1, 0)
    send_y = remote(v_ref.at[pl.ds(0, layer)], halo_y, halo_send.at[1], halo_recv.at[1], 0, 0, -1)
    send_x.start()
    send_y.start()

    n_k = links_ref.shape[1]
    row = iota((layer, layer), 0)
    col = iota((layer, layer), 1)
    same_site = row // 6 == col // 6
    shift = ones_where(col == lax.rem(row + 6, layer)).astype(BF16)
    shift_back = ones_where(row == lax.rem(col + 6, layer)).astype(BF16)
    turn = (
        ones_where((row % 2 == 1) & (col == row - 1)) - ones_where((row % 2 == 0) & (col == row + 1))
    ).astype(BF16)
    pick = ones_where(iota((layer, cells_z), 0) // 6 == iota((layer, cells_z), 1))
    k_row = iota((layer, n_k), 0)
    k_col = iota((layer, n_k), 1)
    color_of_row = (k_row // 2) % 3
    keep_row = color_of_row == (k_col // 6) % 3
    keep_col = color_of_row == (k_col // 2) % 3
    k = iota((n_k, layer), 0)
    c = iota((n_k, layer), 1)
    even = row % 2 == 0

    z_coord = iota((cells_z, 128), 0).astype(F32)
    for mom in range(3):
        angle = (2.0 * math.pi * mom) * z_coord / cells_z
        cos_ref[mom] = jnp.dot(pick, jnp.cos(angle), precision=lax.Precision.HIGHEST, preferred_element_type=F32)
        sin_ref[mom] = jnp.dot(pick, jnp.sin(angle), precision=lax.Precision.HIGHEST, preferred_element_type=F32)

    def put(code, y, plain, rotated):
        field[code, pl.ds(y * layer, layer)] = plain
        turned[code, pl.ds(y * layer, layer)] = rotated

    pick_b = pick.astype(BF16)
    forward = []
    for y in range(cells_y):
        v_y = v_ref[pl.ds(y * layer, layer), :]
        v_turned = mm(turn, v_y)
        put(6, y, v_y.astype(F32), v_turned)
        entries = mm_nt(pick_b, links_ref[y])
        by_row = jnp.where(keep_row, entries, 0.0).astype(BF16)
        by_col = jnp.where(keep_col, entries, 0.0).astype(BF16)
        for d in range(3):
            in_d = k // 18 == d
            re_k, im_k = k % 2 == 0, k % 2 == 1
            re_c, im_c = c % 2 == 0, c % 2 == 1
            b_match = in_d & ((k // 2) % 3 == (c // 2) % 3)
            a_match = in_d & ((k // 6) % 3 == (c // 2) % 3)
            g_re = ones_where(b_match & re_c & re_k) - ones_where(b_match & im_c & im_k)
            g_im = ones_where(b_match & re_c & im_k) + ones_where(b_match & im_c & re_k)
            h_re = ones_where(a_match & re_c & re_k) + ones_where(a_match & im_c & im_k)
            h_im = ones_where(a_match & im_c & re_k) - ones_where(a_match & re_c & im_k)
            q_re = mm(by_row, g_re.astype(BF16))
            q_im = mm(by_row, g_im.astype(BF16))
            apply = jnp.where(same_site, jnp.where(even, q_re, q_im), 0.0).astype(BF16)
            apply_turned = jnp.where(same_site, jnp.where(even, -q_im, q_re), 0.0).astype(BF16)
            p_re = mm(by_col, h_re.astype(BF16))
            p_im = mm(by_col, h_im.astype(BF16))
            adjoint = jnp.where(same_site, jnp.where(even, p_re, p_im), 0.0).astype(BF16)
            carried = mm(adjoint, v_y).astype(BF16)
            if d == 2:
                carried = mm(shift_back, carried).astype(BF16)
                v_next = mm(shift, v_y).astype(BF16)
                put(2, y, mm(apply, v_next), mm(apply_turned, v_next))
            else:
                forward.append((d, y, apply, apply_turned))
            put(3 + d, y, carried.astype(F32), mm(turn, carried))

    vectors = v_ref.shape[1]
    unit = ones_where(iota((vectors, vectors), 0) == iota((vectors, vectors), 1)).astype(BF16)
    left[0] = mm_nt(unit, v_ref[...]).astype(BF16)

    send_y.wait_recv()
    send_x.wait_recv()
    v_y_next = [v_ref[pl.ds(y * layer, layer), :] for y in range(1, cells_y)] + [halo_y[...]]
    left[1] = mm_nt(unit, halo_x[...]).astype(BF16)
    left[2] = mm_nt(unit, jnp.concatenate(v_y_next, axis=0)).astype(BF16)
    for d, y, apply, apply_turned in forward:
        v_next = halo_x[pl.ds(y * layer, layer), :] if d == 0 else v_y_next[y]
        put(d, y, mm(apply, v_next), mm(apply_turned, v_next))

    chunk = vectors // 4
    sends = []
    for j in [i for i in (4, 5, 3, 2, 6, 1, 7, 0) if i < n_gy]:
        op = lax.rem(gy + j, n_gy)
        code = dirs_ref[op]
        mom = moms_ref[op]
        side = jnp.where(code == 3, 1, jnp.where(code == 4, 2, 0))
        cosine = jnp.concatenate([cos_ref[mom]] * cells_y, axis=0)
        sine = jnp.concatenate([sin_ref[mom]] * cells_y, axis=0)
        plain, rotated = field[code], turned[code]
        displaced = (cosine * plain + sine * rotated).astype(BF16)
        minus_turned = (sine * plain - cosine * rotated).astype(BF16)
        right = jnp.concatenate([displaced, minus_turned], axis=1)
        part[j] = mm(left[side], right).reshape(4, chunk, 2 * vectors)
        for i, delta in enumerate(DELTAS):
            if j == 0 and delta == 0:
                continue
            slot = j * 4 + i
            to_chunk = lax.rem(gx + delta % n_gx, 4)
            copy = remote(
                part.at[j, to_chunk], recv.at[slot], part_send.at[slot], part_recv.at[slot], 0, delta, j
            )
            copy.start()
            sends.append(copy)

    summed = part[0, lax.rem(gx, 4)]
    for copy, slot in zip(sends, [s for j in (4, 5, 3, 2, 6, 1, 7, 0) if j < n_gy for s in range(4 * j, 4 * j + 4) if s != 1]):
        copy.wait_recv()
        summed = summed + recv[slot]
    total[...] = summed

    relays = []
    for i in range(n_relay):
        step = 2 if i == 0 else 4
        for way, ring in ((1, relay_r), (-1, relay_l)):
            at = 2 * i + (way < 0)
            if i > 0:
                relays[2 * (i - 1) + (way < 0)].wait_recv()
            copy = remote(
                total if i == 0 else ring.at[i - 1], ring.at[i], relay_send.at[at], relay_recv.at[at], 0, way * step, 0
            )
            copy.start()
            relays.append(copy)
    relays[-2].wait_recv()
    relays[-1].wait_recv()
    final = relay_r[0] + relay_l[0]
    for i in range(1, n_relay):
        final = final + (relay_r[i] + relay_l[i])
    my_chunk = lax.rem(gx + 2, 4)
    every[ta, my_chunk] = (final * norm_factor).astype(BF16)

    lasts = []
    for jt in [i for i in (2, 1, 3, 0) if i < n_ta]:
        for i, delta in enumerate(DELTAS):
            if jt == 0 and delta == 0:
                continue
            slot = jt * 4 + i
            copy = remote(
                every.at[ta, my_chunk], every.at[ta, my_chunk], last_send.at[slot], last_recv.at[slot], jt, delta, 0
            )
            copy.start()
            lasts.append(copy)
    tau_copy.wait()
    for copy in lasts:
        copy.wait_recv()

    mine = every[ta].reshape(vectors, 2 * vectors).astype(F32)
    margin_ref[0] = mine[:, :vectors]
    margin_ref[1] = mine[:, vectors:]

    sink = every[pair_ref[0, 0]].reshape(vectors, 2 * vectors)
    source = every[pair_ref[0, 1]].reshape(vectors, 2 * vectors)
    sink_r, sink_i = sink[:, :vectors], sink[:, vectors:]
    source_r, source_i = source[:, :vectors], source[:, vectors:]
    phi = jnp.concatenate(
        [jnp.concatenate([sink_r, -sink_i], axis=1), jnp.concatenate([sink_i, sink_r], axis=1)], axis=0
    )
    psi = jnp.concatenate([source, jnp.concatenate([-source_i, source_r], axis=1)], axis=0)
    spins = tau_ref.shape[1] // vectors
    x_blocks = []
    for s in range(spins):
        rows = pl.ds(s * vectors, vectors)
        x_blocks.append(mm(phi, jnp.concatenate([tau_ref[0, rows, :], tau_ref[1, rows, :]], axis=0)))
    sum_re = jnp.zeros((vectors, vectors), F32)
    sum_im = jnp.zeros((vectors, vectors), F32)
    for t in range(spins):
        cols = pl.ds(t * vectors, vectors)
        y_block = mm_nt(jnp.concatenate([tau_ref[0, :, cols], tau_ref[1, :, cols]], axis=1), psi)
        for s in range(spins):
            x_re = x_blocks[s][:vectors, t * vectors : (t + 1) * vectors]
            x_im = x_blocks[s][vectors:, t * vectors : (t + 1) * vectors]
            y_re = y_block[s * vectors : (s + 1) * vectors, :vectors]
            y_im = y_block[s * vectors : (s + 1) * vectors, vectors:]
            sum_re = sum_re + (x_re * y_re + x_im * y_im)
            sum_im = sum_im + (x_im * y_re - x_re * y_im)
    corr_ref[0, 0] = jnp.sum(sum_re) / vectors
    corr_ref[0, 1] = jnp.sum(sum_im) / vectors

    for copy in [send_x, send_y] + sends + relays + lasts:
        copy.wait_send()


def solution(mesh):
    sizes = tuple(mesh.shape[axis] for axis in ("ta", "gx", "gy"))

    def per_device(eigvecs, links, op_dirs, op_moms, perams, pair_times, slot_counts):
        cells_x, cells_y, cells_z, colors, parts, vectors = eigvecs.shape[1:]
        rows = cells_x * cells_y * cells_z * colors * parts
        order = perams.shape[-1]
        n_k = 3 * 2 * 3 * 3
        field = eigvecs.reshape(rows, vectors)
        link_rows = links[0, 0].transpose(0, 2, 4, 5, 3, 1).reshape(cells_y, n_k, cells_z)
        norm_factor = 1.0 / math.sqrt(3.0 * cells_x * sizes[1] * cells_y * sizes[2] * cells_z)
        layer = rows // cells_y
        n_relay = sizes[1] // 8
        chunk = vectors // 4
        smem = pl.BlockSpec(memory_space=pltpu.SMEM)
        vmem = pl.BlockSpec(memory_space=pltpu.VMEM)
        dma = pltpu.SemaphoreType.DMA
        margins, corr = pl.pallas_call(
            lambda *refs: kernel(sizes, cells_z, norm_factor, *refs),
            name="meson_step",
            out_shape=(
                jax.ShapeDtypeStruct((2, vectors, vectors), F32),
                jax.ShapeDtypeStruct((1, 2), F32),
            ),
            in_specs=[smem, smem, smem, vmem, vmem, pl.BlockSpec(memory_space=pl.ANY)],
            out_specs=(vmem, smem),
            scratch_shapes=[
                pltpu.VMEM((2, order, order), BF16),
                pltpu.VMEM((rows, vectors), BF16),
                pltpu.VMEM((layer, vectors), BF16),
                pltpu.VMEM((7, rows, vectors), F32),
                pltpu.VMEM((7, rows, vectors), F32),
                pltpu.VMEM((3, vectors, rows), BF16),
                pltpu.VMEM((3, layer, vectors), F32),
                pltpu.VMEM((3, layer, vectors), F32),
                pltpu.VMEM((sizes[2], 4, chunk, 2 * vectors), F32),
                pltpu.VMEM((sizes[2] * 4, chunk, 2 * vectors), F32),
                pltpu.VMEM((chunk, 2 * vectors), F32),
                pltpu.VMEM((n_relay, chunk, 2 * vectors), F32),
                pltpu.VMEM((n_relay, chunk, 2 * vectors), F32),
                pltpu.VMEM((sizes[0], 4, chunk, 2 * vectors), BF16),
                dma,
                dma((2,)),
                dma((2,)),
                dma((sizes[2] * 4,)),
                dma((sizes[2] * 4,)),
                dma((2 * n_relay,)),
                dma((2 * n_relay,)),
                dma((sizes[0] * 4,)),
                dma((sizes[0] * 4,)),
            ],
            compiler_params=pltpu.CompilerParams(collective_id=0, has_side_effects=True),
        )(op_dirs, op_moms, pair_times, field, link_rows, perams[0])
        return margins[None, None], corr[None]

    placed = (
        P("ta", "gx", "gy", None, None, None, None),
        P("ta", "gx", "gy", None, None, None, None, None),
        P(),
        P(),
        P(("ta", "gx"), None, None, None),
        P(("ta", "gx"), None),
        P(("ta", "gx")),
    )
    return jax.shard_map(
        per_device,
        mesh=mesh,
        in_specs=placed,
        out_specs=(P("ta", "gy", None, None, None), P(("ta", "gx"), "gy", None)),
        check_vma=False,
    )
```

time: 753 us -> 83.2 us (0.11)
  the two profiles are of different devices: /device:TPU:24 before, /device:TPU:8 now
where the time goes in v1:
time: 83.2 us; the launch traced here: 82.9 us
  Pallas kernels  78.8 us (95%)
  local copies, waits for them, and re-layouts  3.47 us (4%)
    pallas_call x1, Pallas kernels, per_device(): pl.pallas_call(lambda *refs: kernel(sizes, cells_z, norm_factor, *refs),...  78.8 us
    unnamed x4, local copies, waits for them, and re-layouts  2.08 us

profile of v1, /device:TPU:8, one launch (start us, length us, event | category | flops | bytes accessed | tf_op | source)
XLA Modules:
  0.0 82.9 jit_solution(6459740768961896036)
XLA Ops:
  0.6 0.8 copy.8
  1.4 0.6 copy.9.refs_4_
  2.0 78.8 %meson_step.1 = (f32[2,128,128]{2,1,0:T(8,128)}, f32[1,2]{1,0:T(1,128)}) custom-call(s32[8]{0:T(128)} %refs_0_.1, s32[8]{0:T(128)} %refs_1_.1, s32[1,2]{1,0:T(1,128)} %refs_2_.1, bf16[288,128]{1,0:T(8,128)(2,1)} %bitcast.11, bf16[2,54,24]{2,1,0:T(8,128)(2,1)} %copy.9.refs_4_, bf16[2,512,512]{2,1,0:T(8,128)(2,1)} %bitcast.8), custom_call_target="tpu_custom_call" | custom-call | tf_op jit(solution)/shard_map/meson_step/pallas_call | solution.py:285
  80.8 0.0 copy-start
  80.8 1.6 %copy.12 = f32[1,1,2,128,128]{4,3,2,1,0:T(8,128)} copy(f32[1,1,2,128,128]{4,3,2,1,0:T(8,128)} %bitcast.9) | data formatting | bytes 262144
  82.4 0.0 copy-done
  82.4 0.5 copy.13
Async XLA Ops:
  80.8 1.6 %copy-start = (f32[1,2]{1,0:T(1,128)S(1)}, f32[1,2]{1,0:T(1,128)}, u32[]{:S(2)}) copy-start(f32[1,2]{1,0:T(1,128)} %get-tuple-element.5) | copy-start | bytes 28

commit v2 on v1

--- a/solution.py
+++ b/solution.py
@@ -9,6 +9,7 @@
 
 MESH = pl.DeviceIdType.MESH
 DELTAS = (-1, 0, 1, 2)
+WIDE = (-4, -3, -2, -1, 0, 1, 2, 3)
 F32 = jnp.float32
 BF16 = jnp.bfloat16
 
@@ -32,11 +33,10 @@
 def peers(sizes):
     n_ta, n_gx, n_gy = sizes
     wanted = [(0, -1, 0), (0, 0, -1)]
-    wanted += [(0, delta, j) for j in range(n_gy) for delta in DELTAS]
-    wanted += [(0, step, 0) for step in (2, -2)]
-    if n_gx > 8:
-        wanted += [(0, step, 0) for step in (4, -4)]
-    wanted += [(jt, delta, 0) for jt in range(n_ta) for delta in DELTAS]
+    wanted += [(0, 0, step) for step in (2, -2)]
+    wanted += [(0, delta, step) for step in (0, 2, -2) for delta in DELTAS]
+    wanted += [(0, step, 0) for step in (2, -2, 4, -4)]
+    wanted += [(jt, delta, 0) for jt in range(n_ta) for delta in WIDE]
     seen = []
     for ta, gx, gy in wanted:
         at = (ta % n_ta, gx % n_gx, gy % n_gy)
@@ -47,22 +47,26 @@
 
 def kernel(
     sizes, cells_z, norm_factor,
-    dirs_ref, moms_ref, pair_ref, v_ref, links_ref, perams_ref,
+    dirs_ref, moms_ref, pair_ref, v_hbm, links_hbm, perams_ref,
     margin_ref, corr_ref,
-    tau_ref, halo_x, halo_y, field, turned, left, cos_ref, sin_ref, part, recv, total, relay_r, relay_l, every,
-    tau_sem, halo_send, halo_recv, part_send, part_recv, relay_send, relay_recv, last_send, last_recv,
+    tau_ref, v_ref, links_ref, entry_ref, halo_x, halo_y, field, turned, left, cos_ref, sin_ref,
+    pair_out, pair_in, part, around_in, around, recv, total, half_in, window, far_in, every,
+    local_sem, near_token, far_token, halo_send, halo_recv, pair_send, pair_recv, around_send, around_recv,
+    part_send, part_recv, half_send, half_recv, far_send, far_recv, last_send, last_recv,
 ):
     n_ta, n_gx, n_gy = sizes
     ta, gx, gy = (lax.axis_index(axis) for axis in ("ta", "gx", "gy"))
-    layer = cells_z * 6
-    cells_y = v_ref.shape[0] // layer
-    n_relay = n_gx // 8
+    cells_y = links_ref.shape[0]
+    layer = v_ref.shape[0] // cells_y
+    core = lax.rem(gy, 2)
+    flip = 1 - 2 * core
+    far = n_gx >= 32
 
     def device(dta, dgx, dgy):
         return {
             "ta": lax.rem(ta + dta % n_ta, n_ta),
             "gx": lax.rem(gx + dgx % n_gx, n_gx),
-            "gy": lax.rem(gy + dgy % n_gy, n_gy),
+            "gy": lax.rem(gy + dgy % n_gy, n_gy) if isinstance(dgy, int) else gy + dgy,
         }
 
     def remote(src, dst, send_sem, recv_sem, *offset):
@@ -73,20 +77,36 @@
 
     barrier = pltpu.get_barrier_semaphore()
     known = peers(sizes)
+    pl.semaphore_signal(barrier, inc=1, device_id=device(0, 0, flip), device_id_type=MESH)
     for dta, dgx, dgy in known:
         pl.semaphore_signal(
             barrier, inc=1, device_id=device(-dta, -dgx, -dgy), device_id_type=MESH
         )
-    tau_copy = pltpu.make_async_copy(perams_ref, tau_ref, tau_sem)
-    tau_copy.start()
-
-    pl.semaphore_wait(barrier, len(known))
+    locals_ = [
+        pltpu.make_async_copy(src, dst, local_sem.at[i])
+        for i, (src, dst) in enumerate(
+            ((links_hbm, links_ref), (v_hbm, v_ref), (perams_ref, tau_ref))
+        )
+    ]
+    for copy in locals_:
+        copy.start()
+    locals_[0].wait()
+    locals_[1].wait()
+
+    pl.semaphore_wait(barrier, len(known) + 1)
     send_x = remote(v_ref, halo_x, halo_send.at[0], halo_recv.at[0], 0, -1, 0)
     send_y = remote(v_ref.at[pl.ds(0, layer)], halo_y, halo_send.at[1], halo_recv.at[1], 0, 0, -1)
     send_x.start()
     send_y.start()
-
-    n_k = links_ref.shape[1]
+    if far:
+        for i, step in enumerate((4, -4)):
+            pl.semaphore_signal(near_token.at[i], inc=1, device_id=device(0, step, 0), device_id_type=MESH)
+
+    for y in range(cells_y):
+        for k in range(links_ref.shape[1]):
+            entry_ref[y, pl.ds(2 * k, 2), :] = links_ref[y, k].astype(F32)
+
+    n_k = entry_ref.shape[1]
     row = iota((layer, layer), 0)
     col = iota((layer, layer), 1)
     same_site = row // 6 == col // 6
@@ -121,7 +141,7 @@
         v_y = v_ref[pl.ds(y * layer, layer), :]
         v_turned = mm(turn, v_y)
         put(6, y, v_y.astype(F32), v_turned)
-        entries = mm_nt(pick_b, links_ref[y])
+        entries = mm_nt(pick_b, entry_ref[y].astype(BF16))
         by_row = jnp.where(keep_row, entries, 0.0).astype(BF16)
         by_col = jnp.where(keep_col, entries, 0.0).astype(BF16)
         for d in range(3):
@@ -163,10 +183,17 @@
         v_next = halo_x[pl.ds(y * layer, layer), :] if d == 0 else v_y_next[y]
         put(d, y, mm(apply, v_next), mm(apply_turned, v_next))
 
+    if far:
+        for i, step in enumerate((4, -4)):
+            pl.semaphore_wait(near_token.at[i], 1)
+        for i, step in enumerate((8, -8)):
+            pl.semaphore_signal(far_token.at[i], inc=1, device_id=device(0, step, 0), device_id_type=MESH)
+
     chunk = vectors // 4
-    sends = []
-    for j in [i for i in (4, 5, 3, 2, 6, 1, 7, 0) if i < n_gy]:
-        op = lax.rem(gy + j, n_gy)
+    n_y = n_gy // 2
+    row_y = gy // 2
+
+    def margin(op):
         code = dirs_ref[op]
         mom = moms_ref[op]
         side = jnp.where(code == 3, 1, jnp.where(code == 4, 2, 0))
@@ -176,60 +203,102 @@
         displaced = (cosine * plain + sine * rotated).astype(BF16)
         minus_turned = (sine * plain - cosine * rotated).astype(BF16)
         right = jnp.concatenate([displaced, minus_turned], axis=1)
-        part[j] = mm(left[side], right).reshape(4, chunk, 2 * vectors)
-        for i, delta in enumerate(DELTAS):
-            if j == 0 and delta == 0:
-                continue
-            slot = j * 4 + i
-            to_chunk = lax.rem(gx + delta % n_gx, 4)
-            copy = remote(
-                part.at[j, to_chunk], recv.at[slot], part_send.at[slot], part_recv.at[slot], 0, delta, j
-            )
-            copy.start()
-            sends.append(copy)
-
-    summed = part[0, lax.rem(gx, 4)]
-    for copy, slot in zip(sends, [s for j in (4, 5, 3, 2, 6, 1, 7, 0) if j < n_gy for s in range(4 * j, 4 * j + 4) if s != 1]):
+        return mm(left[side], right).reshape(4, chunk, 2 * vectors)
+
+    order = (2, 1, 3, 0)
+    pairs = {}
+    for k in order:
+        pair_out[k] = margin(2 * lax.rem(row_y + k, n_y) + 1 - core)
+        pairs[k] = remote(pair_out.at[k], pair_in.at[k], pair_send.at[k], pair_recv.at[k], 0, 0, flip)
+        pairs[k].start()
+    for k in order:
+        part[k] = margin(2 * lax.rem(row_y + k, n_y) + core)
+
+    def of(delta):
+        return lax.rem(gx + delta % n_gx, 4)
+
+    sends = {}
+
+    def send_part(src, way, i):
+        slot = way * 4 + i
+        copy = remote(
+            src, recv.at[slot], part_send.at[slot], part_recv.at[slot], 0, DELTAS[i], (0, 2, -2)[way]
+        )
+        copy.start()
+        sends[slot] = copy
+
+    arounds = []
+    for k in order:
+        pairs[k].wait_recv()
+        part[k] = part[k] + pair_in[k]
+        if k == 2:
+            for i in range(4):
+                copy = remote(
+                    part.at[2, of(DELTAS[i])], around_in.at[i], around_send.at[i], around_recv.at[i], 0, 0, 2 if i < 2 else -2
+                )
+                copy.start()
+                arounds.append(copy)
+        elif k == 1:
+            send_part(part.at[1, of(DELTAS[3])], 1, 3)
+            send_part(part.at[1, of(DELTAS[2])], 1, 2)
+        elif k == 3:
+            send_part(part.at[3, of(DELTAS[0])], 2, 0)
+            send_part(part.at[3, of(DELTAS[1])], 2, 1)
+        else:
+            for i in (3, 0, 2):
+                send_part(part.at[0, of(DELTAS[i])], 0, i)
+    for i in (0, 3, 1, 2):
+        arounds[i].wait_recv()
+        around[i] = part[1 if i < 2 else 3, of(DELTAS[i])] + around_in[i]
+        send_part(around.at[i], 1 if i < 2 else 2, i)
+
+    summed = part[0, of(0)]
+    for slot in (3, 0, 2, 7, 6, 8, 9, 4, 11, 5, 10):
+        sends[slot].wait_recv()
+        summed = summed + recv[slot]
+    total[...] = summed.reshape(2, chunk // 2, 2 * vectors)
+
+    halves = []
+    for i, step in enumerate((2, -2)):
+        sub = lax.rem(lax.rem(gx + step % n_gx, n_gx) // 4, 2)
+        copy = remote(total.at[sub], half_in.at[i], half_send.at[i], half_recv.at[i], 0, step, 0)
+        copy.start()
+        halves.append(copy)
+    if far:
+        for i in range(2):
+            pl.semaphore_wait(far_token.at[i], 1)
+    for copy in halves:
         copy.wait_recv()
-        summed = summed + recv[slot]
-    total[...] = summed
-
-    relays = []
-    for i in range(n_relay):
-        step = 2 if i == 0 else 4
-        for way, ring in ((1, relay_r), (-1, relay_l)):
-            at = 2 * i + (way < 0)
-            if i > 0:
-                relays[2 * (i - 1) + (way < 0)].wait_recv()
-            copy = remote(
-                total if i == 0 else ring.at[i - 1], ring.at[i], relay_send.at[at], relay_recv.at[at], 0, way * step, 0
-            )
-            copy.start()
-            relays.append(copy)
-    relays[-2].wait_recv()
-    relays[-1].wait_recv()
-    final = relay_r[0] + relay_l[0]
-    for i in range(1, n_relay):
-        final = final + (relay_r[i] + relay_l[i])
-    my_chunk = lax.rem(gx + 2, 4)
-    every[ta, my_chunk] = (final * norm_factor).astype(BF16)
+    window[...] = half_in[0] + half_in[1]
+    fars = []
+    for i, step in enumerate((12, -12, 4, -4) if far else (4, -4)):
+        copy = remote(window, far_in.at[i], far_send.at[i], far_recv.at[i], 0, step, 0)
+        copy.start()
+        fars.append(copy)
+    for copy in fars[::-1]:
+        copy.wait_recv()
+    final = far_in[0] + far_in[1]
+    for i in range(2, len(fars)):
+        final = final + far_in[i]
+    own = 2 * lax.rem(gx + 2, 4) + lax.rem(gx // 4 + 1, 2)
+    every[ta, own] = (final * norm_factor).astype(BF16)
 
     lasts = []
     for jt in [i for i in (2, 1, 3, 0) if i < n_ta]:
-        for i, delta in enumerate(DELTAS):
-            if jt == 0 and delta == 0:
+        for i in (0, 1, 7, 2, 6, 3, 5, 4):
+            if jt == 0 and WIDE[i] == 0:
                 continue
-            slot = jt * 4 + i
+            slot = jt * 8 + i
             copy = remote(
-                every.at[ta, my_chunk], every.at[ta, my_chunk], last_send.at[slot], last_recv.at[slot], jt, delta, 0
+                every.at[ta, own], every.at[ta, own], last_send.at[slot], last_recv.at[slot], jt, WIDE[i], 0
             )
             copy.start()
             lasts.append(copy)
-    tau_copy.wait()
+    locals_[2].wait()
     for copy in lasts:
         copy.wait_recv()
 
-    mine = every[ta].reshape(vectors, 2 * vectors).astype(F32)
+    mine = every[ta].reshape(vectors, 2 * vectors)
     margin_ref[0] = mine[:, :vectors]
     margin_ref[1] = mine[:, vectors:]
 
@@ -261,7 +330,7 @@
     corr_ref[0, 0] = jnp.sum(sum_re) / vectors
     corr_ref[0, 1] = jnp.sum(sum_im) / vectors
 
-    for copy in [send_x, send_y] + sends + relays + lasts:
+    for copy in [send_x, send_y, *pairs.values(), *arounds, *sends.values(), *halves, *fars, *lasts]:
         copy.wait_send()
 
 
@@ -274,25 +343,31 @@
         order = perams.shape[-1]
         n_k = 3 * 2 * 3 * 3
         field = eigvecs.reshape(rows, vectors)
-        link_rows = links[0, 0].transpose(0, 2, 4, 5, 3, 1).reshape(cells_y, n_k, cells_z)
+        link_rows = links[0, 0].transpose(0, 2, 4, 5, 3, 1).reshape(cells_y, n_k // 2, 2, cells_z)
         norm_factor = 1.0 / math.sqrt(3.0 * cells_x * sizes[1] * cells_y * sizes[2] * cells_z)
         layer = rows // cells_y
-        n_relay = sizes[1] // 8
+        n_far = 4 if sizes[1] >= 32 else 2
         chunk = vectors // 4
+        piece = (chunk, 2 * vectors)
+        half = (chunk // 2, 2 * vectors)
         smem = pl.BlockSpec(memory_space=pltpu.SMEM)
         vmem = pl.BlockSpec(memory_space=pltpu.VMEM)
+        hbm = pl.BlockSpec(memory_space=pl.ANY)
         dma = pltpu.SemaphoreType.DMA
         margins, corr = pl.pallas_call(
             lambda *refs: kernel(sizes, cells_z, norm_factor, *refs),
             name="meson_step",
             out_shape=(
-                jax.ShapeDtypeStruct((2, vectors, vectors), F32),
+                jax.ShapeDtypeStruct((2, vectors, vectors), BF16),
                 jax.ShapeDtypeStruct((1, 2), F32),
             ),
-            in_specs=[smem, smem, smem, vmem, vmem, pl.BlockSpec(memory_space=pl.ANY)],
+            in_specs=[smem, smem, smem, hbm, hbm, hbm],
             out_specs=(vmem, smem),
             scratch_shapes=[
                 pltpu.VMEM((2, order, order), BF16),
+                pltpu.VMEM((rows, vectors), BF16),
+                pltpu.VMEM((cells_y, n_k // 2, 2, cells_z), BF16),
+                pltpu.VMEM((cells_y, n_k, cells_z), F32),
                 pltpu.VMEM((rows, vectors), BF16),
                 pltpu.VMEM((layer, vectors), BF16),
                 pltpu.VMEM((7, rows, vectors), F32),
@@ -300,25 +375,38 @@
                 pltpu.VMEM((3, vectors, rows), BF16),
                 pltpu.VMEM((3, layer, vectors), F32),
                 pltpu.VMEM((3, layer, vectors), F32),
-                pltpu.VMEM((sizes[2], 4, chunk, 2 * vectors), F32),
-                pltpu.VMEM((sizes[2] * 4, chunk, 2 * vectors), F32),
-                pltpu.VMEM((chunk, 2 * vectors), F32),
-                pltpu.VMEM((n_relay, chunk, 2 * vectors), F32),
-                pltpu.VMEM((n_relay, chunk, 2 * vectors), F32),
-                pltpu.VMEM((sizes[0], 4, chunk, 2 * vectors), BF16),
-                dma,
+                pltpu.VMEM((4, 4, *piece), F32),
+                pltpu.VMEM((4, 4, *piece), F32),
+                pltpu.VMEM((4, 4, *piece), F32),
+                pltpu.VMEM((4, *piece), F32),
+                pltpu.VMEM((4, *piece), F32),
+                pltpu.VMEM((12, *piece), F32),
+                pltpu.VMEM((2, *half), F32),
+                pltpu.VMEM((2, *half), F32),
+                pltpu.VMEM(half, F32),
+                pltpu.VMEM((n_far, *half), F32),
+                pltpu.VMEM((sizes[0], 8, *half), BF16),
+                dma((3,)),
+                pltpu.SemaphoreType.REGULAR((2,)),
+                pltpu.SemaphoreType.REGULAR((2,)),
                 dma((2,)),
                 dma((2,)),
-                dma((sizes[2] * 4,)),
-                dma((sizes[2] * 4,)),
-                dma((2 * n_relay,)),
-                dma((2 * n_relay,)),
-                dma((sizes[0] * 4,)),
-                dma((sizes[0] * 4,)),
+                dma((4,)),
+                dma((4,)),
+                dma((4,)),
+                dma((4,)),
+                dma((12,)),
+                dma((12,)),
+                dma((2,)),
+                dma((2,)),
+                dma((n_far,)),
+                dma((n_far,)),
+                dma((sizes[0] * 8,)),
+                dma((sizes[0] * 8,)),
             ],
             compiler_params=pltpu.CompilerParams(collective_id=0, has_side_effects=True),
         )(op_dirs, op_moms, pair_times, field, link_rows, perams[0])
-        return margins[None, None], corr[None]
+        return margins.astype(F32)[None, None], corr[None]
 
     placed = (
         P("ta", "gx", "gy", None, None, None, None),

time: 83.2 us -> 66.3 us (0.80)
  the two profiles are of different devices: /device:TPU:8 before, /device:TPU:24 now
where the time goes in v2:
time: 66.3 us; the launch traced here: 65.2 us
  Pallas kernels  62.6 us (94%)
  other arithmetic  1.5 us (2%)
    pallas_call x1, Pallas kernels, per_device(): pl.pallas_call(lambda *refs: kernel(sizes, cells_z, norm_factor, *refs),...  62.6 us
    broadcast_in_dim x1, other arithmetic, per_device(): return (margins.astype(F32)[None, None], corr[None])  1.5 us

profile of v2, /device:TPU:24, one launch (start us, length us, event | category | flops | bytes accessed | tf_op | source)
XLA Modules:
  0.0 65.2 jit_solution(11429703958858441779)
XLA Ops:
  0.6 62.6 %meson_step.1 = (bf16[2,128,128]{2,1,0:T(8,128)(2,1)}, f32[1,2]{1,0:T(1,128)}) custom-call(s32[8]{0:T(128)} %refs_0_.1, s32[8]{0:T(128)} %refs_1_.1, s32[1,2]{1,0:T(1,128)} %refs_2_.1, bf16[288,128]{1,0:T(8,128)(2,1)} %bitcast.12, bf16[2,27,2,24]{3,2,1,0:T(2,128)(2,1)} %bitcast.13, bf16[2,512,512]{2,1,0:T(8,128)(2,1)} %bitcast.11), custom_call_target="tpu_custom_call" | custom-call | tf_op jit(solution)/shard_map/meson_step/pallas_call | solution.py:357
  63.2 0.0 copy-start
  63.2 1.5 %bitcast_convert_fusion = f32[1,1,2,128,128]{4,3,2,1,0:T(8,128)} fusion(bf16[2,128,128]{2,1,0:T(8,128)(2,1)} %get-tuple-element.4), kind=kLoop, calls=%fused_computation | loop fusion | flops 32768 | bytes 196608 | tf_op jit(solution)/shard_map/broadcast_in_dim | solution.py:409
  64.7 0.0 copy-done
  64.7 0.5 copy.9
Async XLA Ops:
  63.2 1.5 %copy-start = (f32[1,2]{1,0:T(1,128)S(1)}, f32[1,2]{1,0:T(1,128)}, u32[]{:S(2)}) copy-start(f32[1,2]{1,0:T(1,128)} %get-tuple-element.5) | copy-start | bytes 28

commit v3 on v2

--- a/solution.py
+++ b/solution.py
@@ -32,11 +32,7 @@
 
 def peers(sizes):
     n_ta, n_gx, n_gy = sizes
-    wanted = [(0, -1, 0), (0, 0, -1)]
-    wanted += [(0, 0, step) for step in (2, -2)]
-    wanted += [(0, delta, step) for step in (0, 2, -2) for delta in DELTAS]
-    wanted += [(0, step, 0) for step in (2, -2, 4, -4)]
-    wanted += [(jt, delta, 0) for jt in range(n_ta) for delta in WIDE]
+    wanted = [(0, -1, 0), (0, 1, 0), (0, 0, -1), (0, 0, 2), (0, 0, -2), (1, 0, 0), (-1, 0, 0)]
     seen = []
     for ta, gx, gy in wanted:
         at = (ta % n_ta, gx % n_gx, gy % n_gy)
@@ -49,18 +45,20 @@
     sizes, cells_z, norm_factor,
     dirs_ref, moms_ref, pair_ref, v_hbm, links_hbm, perams_ref,
     margin_ref, corr_ref,
-    tau_ref, v_ref, links_ref, entry_ref, halo_x, halo_y, field, turned, left, cos_ref, sin_ref,
-    pair_out, pair_in, part, around_in, around, recv, total, half_in, window, far_in, every,
-    local_sem, near_token, far_token, halo_send, halo_recv, pair_send, pair_recv, around_send, around_recv,
+    tau_ref, v_ref, links_ref, entry_ref, halo_x, field, turned, left, cos_ref, sin_ref,
+    part, around_in, around, recv, total, half_in, window, far_in, every,
+    local_sem, token, halo_send, halo_recv, around_send, around_recv,
     part_send, part_recv, half_send, half_recv, far_send, far_recv, last_send, last_recv,
 ):
     n_ta, n_gx, n_gy = sizes
     ta, gx, gy = (lax.axis_index(axis) for axis in ("ta", "gx", "gy"))
-    cells_y = links_ref.shape[0]
-    layer = v_ref.shape[0] // cells_y
+    cells_y = links_ref.shape[1]
+    rows = v_hbm.shape[0]
+    layer = rows // cells_y
     core = lax.rem(gy, 2)
     flip = 1 - 2 * core
     far = n_gx >= 32
+    mine_at = pl.ds(pl.multiple_of(core * rows, rows), rows)
 
     def device(dta, dgx, dgy):
         return {
@@ -77,7 +75,8 @@
 
     barrier = pltpu.get_barrier_semaphore()
     known = peers(sizes)
-    pl.semaphore_signal(barrier, inc=1, device_id=device(0, 0, flip), device_id_type=MESH)
+    for dgx in (0, 1):
+        pl.semaphore_signal(barrier, inc=1, device_id=device(0, dgx, flip), device_id_type=MESH)
     for dta, dgx, dgy in known:
         pl.semaphore_signal(
             barrier, inc=1, device_id=device(-dta, -dgx, -dgy), device_id_type=MESH
@@ -85,28 +84,12 @@
     locals_ = [
         pltpu.make_async_copy(src, dst, local_sem.at[i])
         for i, (src, dst) in enumerate(
-            ((links_hbm, links_ref), (v_hbm, v_ref), (perams_ref, tau_ref))
+            ((links_hbm, links_ref.at[core]), (v_hbm, v_ref.at[mine_at]), (perams_ref, tau_ref))
         )
     ]
     for copy in locals_:
         copy.start()
-    locals_[0].wait()
-    locals_[1].wait()
-
-    pl.semaphore_wait(barrier, len(known) + 1)
-    send_x = remote(v_ref, halo_x, halo_send.at[0], halo_recv.at[0], 0, -1, 0)
-    send_y = remote(v_ref.at[pl.ds(0, layer)], halo_y, halo_send.at[1], halo_recv.at[1], 0, 0, -1)
-    send_x.start()
-    send_y.start()
-    if far:
-        for i, step in enumerate((4, -4)):
-            pl.semaphore_signal(near_token.at[i], inc=1, device_id=device(0, step, 0), device_id_type=MESH)
-
-    for y in range(cells_y):
-        for k in range(links_ref.shape[1]):
-            entry_ref[y, pl.ds(2 * k, 2), :] = links_ref[y, k].astype(F32)
-
-    n_k = entry_ref.shape[1]
+    n_k = entry_ref.shape[0]
     row = iota((layer, layer), 0)
     col = iota((layer, layer), 1)
     same_site = row // 6 == col // 6
@@ -131,64 +114,127 @@
         cos_ref[mom] = jnp.dot(pick, jnp.cos(angle), precision=lax.Precision.HIGHEST, preferred_element_type=F32)
         sin_ref[mom] = jnp.dot(pick, jnp.sin(angle), precision=lax.Precision.HIGHEST, preferred_element_type=F32)
 
-    def put(code, y, plain, rotated):
-        field[code, pl.ds(y * layer, layer)] = plain
-        turned[code, pl.ds(y * layer, layer)] = rotated
+    def put(code, at, plain, rotated):
+        field[code, at] = plain
+        turned[code, at] = rotated
+
+    maps = []
+    for d in range(3):
+        in_d = k // 18 == d
+        re_k, im_k = k % 2 == 0, k % 2 == 1
+        re_c, im_c = c % 2 == 0, c % 2 == 1
+        b_match = in_d & ((k // 2) % 3 == (c // 2) % 3)
+        a_match = in_d & ((k // 6) % 3 == (c // 2) % 3)
+        g_re = ones_where(b_match & re_c & re_k) - ones_where(b_match & im_c & im_k)
+        g_im = ones_where(b_match & re_c & im_k) + ones_where(b_match & im_c & re_k)
+        h_re = ones_where(a_match & re_c & re_k) + ones_where(a_match & im_c & im_k)
+        h_im = ones_where(a_match & im_c & re_k) - ones_where(a_match & re_c & im_k)
+        maps.append([m.astype(BF16) for m in (g_re, g_im, h_re, h_im)])
+
+    pl.semaphore_wait(barrier, len(known) + 2)
+    halos = [
+        remote(v_hbm, halo_x.at[mine_at], halo_send.at[0], halo_recv.at[0], 0, -1, 0),
+        remote(v_hbm, v_ref.at[mine_at], halo_send.at[1], halo_recv.at[1], 0, 0, flip),
+        remote(links_hbm, links_ref.at[core], halo_send.at[2], halo_recv.at[2], 0, 0, flip),
+        remote(v_hbm, halo_x.at[mine_at], halo_send.at[3], halo_recv.at[3], 0, -1, flip),
+    ]
+    edge = v_hbm.at[pl.ds(0, layer)]
+    edge_to = v_ref.at[pl.ds(2 * rows, layer)]
+    edges = [
+        remote(edge, edge_to, halo_send.at[4 + i], halo_recv.at[4], 0, 0, step)
+        for i, step in enumerate((-1, -2))
+    ]
+    for copy in halos:
+        copy.start()
+
+    @pl.when(core == 0)
+    def _():
+        for copy in edges:
+            copy.start()
+
+    ring = {"a": (0, 1), "b": (2, 2)}
+    if far:
+        ring |= {"c": (4, 4), "d": (6, 8)}
+    side_ways = {"e": 8, "f": 10} if n_ta > 1 else {}
+
+    def tell(name):
+        if name in ring:
+            at, step = ring[name]
+            to = [(at, (0, step, 0)), (at + 1, (0, -step, 0))]
+        else:
+            to = [(side_ways[name] + i, (way, 0, 0)) for i, way in enumerate((1, -1))] if side_ways else []
+        for at, offset in to:
+            pl.semaphore_signal(token.at[at], inc=1, device_id=device(*offset), device_id_type=MESH)
+
+    def heard(name):
+        if name in ring or side_ways:
+            at = ring[name][0] if name in ring else side_ways[name]
+            pl.semaphore_wait(token.at[at], 1)
+            pl.semaphore_wait(token.at[at + 1], 1)
+
+    tell("a")
 
     pick_b = pick.astype(BF16)
     forward = []
-    for y in range(cells_y):
-        v_y = v_ref[pl.ds(y * layer, layer), :]
-        v_turned = mm(turn, v_y)
-        put(6, y, v_y.astype(F32), v_turned)
-        entries = mm_nt(pick_b, entry_ref[y].astype(BF16))
-        by_row = jnp.where(keep_row, entries, 0.0).astype(BF16)
-        by_col = jnp.where(keep_col, entries, 0.0).astype(BF16)
-        for d in range(3):
-            in_d = k // 18 == d
-            re_k, im_k = k % 2 == 0, k % 2 == 1
-            re_c, im_c = c % 2 == 0, c % 2 == 1
-            b_match = in_d & ((k // 2) % 3 == (c // 2) % 3)
-            a_match = in_d & ((k // 6) % 3 == (c // 2) % 3)
-            g_re = ones_where(b_match & re_c & re_k) - ones_where(b_match & im_c & im_k)
-            g_im = ones_where(b_match & re_c & im_k) + ones_where(b_match & im_c & re_k)
-            h_re = ones_where(a_match & re_c & re_k) + ones_where(a_match & im_c & im_k)
-            h_im = ones_where(a_match & im_c & re_k) - ones_where(a_match & re_c & im_k)
-            q_re = mm(by_row, g_re.astype(BF16))
-            q_im = mm(by_row, g_im.astype(BF16))
-            apply = jnp.where(same_site, jnp.where(even, q_re, q_im), 0.0).astype(BF16)
-            apply_turned = jnp.where(same_site, jnp.where(even, -q_im, q_re), 0.0).astype(BF16)
-            p_re = mm(by_col, h_re.astype(BF16))
-            p_im = mm(by_col, h_im.astype(BF16))
-            adjoint = jnp.where(same_site, jnp.where(even, p_re, p_im), 0.0).astype(BF16)
-            carried = mm(adjoint, v_y).astype(BF16)
-            if d == 2:
-                carried = mm(shift_back, carried).astype(BF16)
-                v_next = mm(shift, v_y).astype(BF16)
-                put(2, y, mm(apply, v_next), mm(apply_turned, v_next))
-            else:
-                forward.append((d, y, apply, apply_turned))
-            put(3 + d, y, carried.astype(F32), mm(turn, carried))
+    for own in (True, False):
+        if own:
+            locals_[0].wait()
+            locals_[1].wait()
+        else:
+            heard("a")
+            tell("b")
+            halos[1].wait_recv()
+            halos[2].wait_recv()
+        whose = core if own else 1 - core
+        for y in range(cells_y):
+            at = pl.ds(pl.multiple_of(whose * rows + y * layer, layer), layer)
+            after = pl.ds(pl.multiple_of(whose * rows + (y + 1) * layer, layer), layer)
+            for kk in range(links_ref.shape[2]):
+                entry_ref[pl.ds(2 * kk, 2), :] = links_ref[whose, y, kk].astype(F32)
+            v_y = v_ref[at, :]
+            put(6, at, v_y.astype(F32), mm(turn, v_y))
+            entries = mm_nt(pick_b, entry_ref[...].astype(BF16))
+            by_row = jnp.where(keep_row, entries, 0.0).astype(BF16)
+            by_col = jnp.where(keep_col, entries, 0.0).astype(BF16)
+            for d in range(3):
+                g_re, g_im, h_re, h_im = maps[d]
+                q_re = mm(by_row, g_re)
+                q_im = mm(by_row, g_im)
+                apply = jnp.where(same_site, jnp.where(even, q_re, q_im), 0.0).astype(BF16)
+                apply_turned = jnp.where(same_site, jnp.where(even, -q_im, q_re), 0.0).astype(BF16)
+                p_re = mm(by_col, h_re)
+                p_im = mm(by_col, h_im)
+                adjoint = jnp.where(same_site, jnp.where(even, p_re, p_im), 0.0).astype(BF16)
+                carried = mm(adjoint, v_y).astype(BF16)
+                if d == 2:
+                    carried = mm(shift_back, carried).astype(BF16)
+                    v_next = mm(shift, v_y).astype(BF16)
+                    put(2, at, mm(apply, v_next), mm(apply_turned, v_next))
+                else:
+                    forward.append((d, at, after, apply, apply_turned))
+                put(3 + d, at, carried.astype(F32), mm(turn, carried))
 
     vectors = v_ref.shape[1]
     unit = ones_where(iota((vectors, vectors), 0) == iota((vectors, vectors), 1)).astype(BF16)
-    left[0] = mm_nt(unit, v_ref[...]).astype(BF16)
-
-    send_y.wait_recv()
-    send_x.wait_recv()
-    v_y_next = [v_ref[pl.ds(y * layer, layer), :] for y in range(1, cells_y)] + [halo_y[...]]
+    left[0] = mm_nt(unit, v_ref[pl.ds(0, 2 * rows), :]).astype(BF16)
+
+    edges[0].wait_recv()
+    left[2] = mm_nt(unit, v_ref[pl.ds(layer, 2 * rows), :]).astype(BF16)
+    for d, at, after, apply, apply_turned in forward:
+        if d == 1:
+            v_next = v_ref[after, :]
+            put(1, at, mm(apply, v_next), mm(apply_turned, v_next))
+    halos[0].wait_recv()
+    halos[3].wait_recv()
+    heard("b")
+    if far:
+        tell("c")
+    tell("e")
     left[1] = mm_nt(unit, halo_x[...]).astype(BF16)
-    left[2] = mm_nt(unit, jnp.concatenate(v_y_next, axis=0)).astype(BF16)
-    for d, y, apply, apply_turned in forward:
-        v_next = halo_x[pl.ds(y * layer, layer), :] if d == 0 else v_y_next[y]
-        put(d, y, mm(apply, v_next), mm(apply_turned, v_next))
-
-    if far:
-        for i, step in enumerate((4, -4)):
-            pl.semaphore_wait(near_token.at[i], 1)
-        for i, step in enumerate((8, -8)):
-            pl.semaphore_signal(far_token.at[i], inc=1, device_id=device(0, step, 0), device_id_type=MESH)
-
+    for d, at, after, apply, apply_turned in forward:
+        if d == 0:
+            v_next = halo_x[at, :]
+            put(0, at, mm(apply, v_next), mm(apply_turned, v_next))
     chunk = vectors // 4
     n_y = n_gy // 2
     row_y = gy // 2
@@ -197,8 +243,8 @@
         code = dirs_ref[op]
         mom = moms_ref[op]
         side = jnp.where(code == 3, 1, jnp.where(code == 4, 2, 0))
-        cosine = jnp.concatenate([cos_ref[mom]] * cells_y, axis=0)
-        sine = jnp.concatenate([sin_ref[mom]] * cells_y, axis=0)
+        cosine = jnp.concatenate([cos_ref[mom]] * (2 * cells_y), axis=0)
+        sine = jnp.concatenate([sin_ref[mom]] * (2 * cells_y), axis=0)
         plain, rotated = field[code], turned[code]
         displaced = (cosine * plain + sine * rotated).astype(BF16)
         minus_turned = (sine * plain - cosine * rotated).astype(BF16)
@@ -206,13 +252,6 @@
         return mm(left[side], right).reshape(4, chunk, 2 * vectors)
 
     order = (2, 1, 3, 0)
-    pairs = {}
-    for k in order:
-        pair_out[k] = margin(2 * lax.rem(row_y + k, n_y) + 1 - core)
-        pairs[k] = remote(pair_out.at[k], pair_in.at[k], pair_send.at[k], pair_recv.at[k], 0, 0, flip)
-        pairs[k].start()
-    for k in order:
-        part[k] = margin(2 * lax.rem(row_y + k, n_y) + core)
 
     def of(delta):
         return lax.rem(gx + delta % n_gx, 4)
@@ -229,8 +268,7 @@
 
     arounds = []
     for k in order:
-        pairs[k].wait_recv()
-        part[k] = part[k] + pair_in[k]
+        part[k] = margin(2 * lax.rem(row_y + k, n_y) + core)
         if k == 2:
             for i in range(4):
                 copy = remote(
@@ -247,6 +285,11 @@
         else:
             for i in (3, 0, 2):
                 send_part(part.at[0, of(DELTAS[i])], 0, i)
+    if far:
+        heard("c")
+        tell("d")
+    heard("e")
+    tell("f")
     for i in (0, 3, 1, 2):
         arounds[i].wait_recv()
         around[i] = part[1 if i < 2 else 3, of(DELTAS[i])] + around_in[i]
@@ -265,8 +308,7 @@
         copy.start()
         halves.append(copy)
     if far:
-        for i in range(2):
-            pl.semaphore_wait(far_token.at[i], 1)
+        heard("d")
     for copy in halves:
         copy.wait_recv()
     window[...] = half_in[0] + half_in[1]
@@ -283,6 +325,7 @@
     own = 2 * lax.rem(gx + 2, 4) + lax.rem(gx // 4 + 1, 2)
     every[ta, own] = (final * norm_factor).astype(BF16)
 
+    heard("f")
     lasts = []
     for jt in [i for i in (2, 1, 3, 0) if i < n_ta]:
         for i in (0, 1, 7, 2, 6, 3, 5, 4):
@@ -330,8 +373,13 @@
     corr_ref[0, 0] = jnp.sum(sum_re) / vectors
     corr_ref[0, 1] = jnp.sum(sum_im) / vectors
 
-    for copy in [send_x, send_y, *pairs.values(), *arounds, *sends.values(), *halves, *fars, *lasts]:
+    for copy in [*halos, *arounds, *sends.values(), *halves, *fars, *lasts]:
         copy.wait_send()
+
+    @pl.when(core == 0)
+    def _():
+        for copy in edges:
+            copy.wait_send()
 
 
 def solution(mesh):
@@ -352,31 +400,28 @@
         half = (chunk // 2, 2 * vectors)
         smem = pl.BlockSpec(memory_space=pltpu.SMEM)
         vmem = pl.BlockSpec(memory_space=pltpu.VMEM)
-        hbm = pl.BlockSpec(memory_space=pl.ANY)
+        hbm = pl.BlockSpec(memory_space=pltpu.HBM)
         dma = pltpu.SemaphoreType.DMA
         margins, corr = pl.pallas_call(
             lambda *refs: kernel(sizes, cells_z, norm_factor, *refs),
             name="meson_step",
             out_shape=(
-                jax.ShapeDtypeStruct((2, vectors, vectors), BF16),
+                pltpu.VMEM((2, vectors, vectors), BF16),
                 jax.ShapeDtypeStruct((1, 2), F32),
             ),
             in_specs=[smem, smem, smem, hbm, hbm, hbm],
             out_specs=(vmem, smem),
             scratch_shapes=[
                 pltpu.VMEM((2, order, order), BF16),
-                pltpu.VMEM((rows, vectors), BF16),
-                pltpu.VMEM((cells_y, n_k // 2, 2, cells_z), BF16),
-                pltpu.VMEM((cells_y, n_k, cells_z), F32),
-                pltpu.VMEM((rows, vectors), BF16),
-                pltpu.VMEM((layer, vectors), BF16),
-                pltpu.VMEM((7, rows, vectors), F32),
-                pltpu.VMEM((7, rows, vectors), F32),
-                pltpu.VMEM((3, vectors, rows), BF16),
+                pltpu.VMEM((2 * rows + layer, vectors), BF16),
+                pltpu.VMEM((2, cells_y, n_k // 2, 2, cells_z), BF16),
+                pltpu.VMEM((n_k, cells_z), F32),
+                pltpu.VMEM((2 * rows, vectors), BF16),
+                pltpu.VMEM((7, 2 * rows, vectors), F32),
+                pltpu.VMEM((7, 2 * rows, vectors), F32),
+                pltpu.VMEM((3, vectors, 2 * rows), BF16),
                 pltpu.VMEM((3, layer, vectors), F32),
                 pltpu.VMEM((3, layer, vectors), F32),
-                pltpu.VMEM((4, 4, *piece), F32),
-                pltpu.VMEM((4, 4, *piece), F32),
                 pltpu.VMEM((4, 4, *piece), F32),
                 pltpu.VMEM((4, *piece), F32),
                 pltpu.VMEM((4, *piece), F32),
@@ -387,12 +432,9 @@
                 pltpu.VMEM((n_far, *half), F32),
                 pltpu.VMEM((sizes[0], 8, *half), BF16),
                 dma((3,)),
-                pltpu.SemaphoreType.REGULAR((2,)),
-                pltpu.SemaphoreType.REGULAR((2,)),
-                dma((2,)),
-                dma((2,)),
-                dma((4,)),
-                dma((4,)),
+                pltpu.SemaphoreType.REGULAR((12,)),
+                dma((6,)),
+                dma((5,)),
                 dma((4,)),
                 dma((4,)),
                 dma((12,)),
@@ -404,7 +446,7 @@
                 dma((sizes[0] * 8,)),
                 dma((sizes[0] * 8,)),
             ],
-            compiler_params=pltpu.CompilerParams(collective_id=0, has_side_effects=True),
+            compiler_params=pltpu.CompilerParams(collective_id=0, has_side_effects=True, vmem_limit_bytes=56000 * 1024),
         )(op_dirs, op_moms, pair_times, field, link_rows, perams[0])
         return margins.astype(F32)[None, None], corr[None]
 

time: 66.3 us -> 63.9 us (0.964); the launches traced: 65.2 us -> 63.8 us
  other arithmetic: 1.5 us -> 0.67 us
    broadcast_in_dim x1, other arithmetic: 1.5 us -> 0.67 us  [per_device(): return (margins.astype(F32)[None, None], corr[None])]
where the time goes in v3:
time: 63.9 us; the launch traced here: 63.8 us
  Pallas kernels  62 us (97%)
  other arithmetic  0.67 us (1%)
  between operations  0.65 us (1%)
    pallas_call x1, Pallas kernels, per_device(): pl.pallas_call(lambda *refs: kernel(sizes, cells_z, norm_factor, *refs),...  62 us

profile of v3, /device:TPU:24, one launch (start us, length us, event | category | flops | bytes accessed | tf_op | source)
XLA Modules:
  0.0 63.8 jit_solution(13764278407430723470)
XLA Ops:
  0.6 62.0 %meson_step.1 = (bf16[2,128,128]{2,1,0:T(8,128)(2,1)S(1)}, f32[1,2]{1,0:T(1,128)}) custom-call(s32[8]{0:T(128)} %refs_0_.1, s32[8]{0:T(128)} %refs_1_.1, s32[1,2]{1,0:T(1,128)} %refs_2_.1, bf16[288,128]{1,0:T(8,128)(2,1)} %bitcast.12, bf16[2,27,2,24]{3,2,1,0:T(2,128)(2,1)} %bitcast.13, bf16[2,512,512]{2,1,0:T(8,128)(2,1)} %bitcast.11), custom_call_target="tpu_custom_call" | custom-call | tf_op jit(solution)/shard_map/meson_step/pallas_call | solution.py:405
  62.6 0.0 copy-start
  62.6 0.7 %bitcast_convert_fusion = f32[1,1,2,128,128]{4,3,2,1,0:T(8,128)} fusion(bf16[2,128,128]{2,1,0:T(8,128)(2,1)S(1)} %get-tuple-element.4), kind=kLoop, calls=%fused_computation | loop fusion | flops 32768 | bytes 196608 | tf_op jit(solution)/shard_map/broadcast_in_dim | solution.py:451
  63.3 0.0 copy-done
  63.3 0.5 copy.9
Async XLA Ops:
  62.6 0.7 %copy-start = (f32[1,2]{1,0:T(1,128)S(1)}, f32[1,2]{1,0:T(1,128)}, u32[]{:S(2)}) copy-start(f32[1,2]{1,0:T(1,128)} %get-tuple-element.5) | copy-start | bytes 28

commit v4 on v3

--- a/solution.py
+++ b/solution.py
@@ -2,6 +2,7 @@
 
 import jax
 import jax.numpy as jnp
+import numpy as np
 from jax import lax
 from jax.experimental import pallas as pl
 from jax.experimental.pallas import tpu as pltpu
@@ -14,20 +15,49 @@
 BF16 = jnp.bfloat16
 
 
-def iota(shape, dim):
-    return lax.broadcasted_iota(jnp.int32, shape, dim)
-
-
-def ones_where(cond):
-    return jnp.where(cond, 1.0, 0.0).astype(F32)
-
-
 def mm(a, b):
     return jnp.dot(a, b, preferred_element_type=F32)
 
 
 def mm_nt(a, b):
     return lax.dot_general(a, b, (((1,), (1,)), ((), ())), preferred_element_type=F32)
+
+
+def phases(cells_z, vectors):
+    angle = 2.0 * math.pi * np.arange(3)[:, None] * np.repeat(np.arange(cells_z), 6)[None] / cells_z
+    return [np.repeat(f(angle)[..., None], vectors, axis=2) for f in (np.cos, np.sin)]
+
+
+def selections(cells_z, vectors):
+    layer, block, n_k = cells_z * 6, 48, 54
+    at = np.arange(layer)
+    shift = at[None] == (at[:, None] + 6) % layer
+    r = np.arange(block)
+    turn = ((r[:, None] % 2 == 1) & (r[None] == r[:, None] - 1)) * 1.0
+    turn = turn - ((r[:, None] % 2 == 0) & (r[None] == r[:, None] + 1))
+    same_site = (at[:, None] % block) // 6 == r[None] // 6
+    pick = at[:, None] // 6 == np.arange(cells_z)[None]
+    k = np.arange(2 * n_k) % n_k
+    first = (np.arange(2 * n_k) < n_k)[None]
+    even = (at % 2 == 0)[:, None]
+    color = (at // 2 % 3)[:, None]
+    keep_row, keep_col = color == (k // 6 % 3)[None], color == (k // 2 % 3)[None]
+    row_plain = keep_row & (even == first)
+    row_turned = (keep_row & first & ~even) * 1.0 - (keep_row & ~first & even)
+    col_plain = keep_col & (even == first)
+    maps = []
+    k, first, c = k[:, None], first.T, r[None]
+    re_k, im_k, re_c, im_c = k % 2 == 0, k % 2 == 1, c % 2 == 0, c % 2 == 1
+    for d in range(3):
+        b_match = (k // 18 == d) & (k // 2 % 3 == c // 2 % 3)
+        a_match = (k // 18 == d) & (k // 6 % 3 == c // 2 % 3)
+        g_re = (b_match & re_c & re_k) * 1.0 - (b_match & im_c & im_k)
+        g_im = (b_match & re_c & im_k) * 1.0 + (b_match & im_c & re_k)
+        h_re = (a_match & re_c & re_k) * 1.0 + (a_match & im_c & im_k)
+        h_im = (a_match & im_c & re_k) * 1.0 - (a_match & re_c & im_k)
+        maps += [np.where(first, g_re, g_im), np.where(first, h_re, h_im)]
+    tables = [turn, shift, shift.T, same_site, pick, row_plain, row_turned, col_plain, np.eye(vectors), *maps]
+    return [np.asarray(t, np.float32) for t in tables]
 
 
 def peers(sizes):
@@ -42,14 +72,15 @@
 
 
 def kernel(
-    sizes, cells_z, norm_factor,
-    dirs_ref, moms_ref, pair_ref, v_hbm, links_hbm, perams_ref,
-    margin_ref, corr_ref,
-    tau_ref, v_ref, links_ref, entry_ref, halo_x, field, turned, left, cos_ref, sin_ref,
-    part, around_in, around, recv, total, half_in, window, far_in, every,
-    local_sem, token, halo_send, halo_recv, around_send, around_recv,
-    part_send, part_recv, half_send, half_recv, far_send, far_recv, last_send, last_recv,
+    sizes, n_tables, norm_factor,
+    dirs_hbm, moms_hbm, pair_hbm, v_hbm, links_hbm, perams_ref, *rest,
 ):
+    sources, (margin_ref, corr_ref) = rest[:n_tables], rest[n_tables : n_tables + 2]
+    tables, rest = rest[n_tables + 2 : 2 * n_tables + 2], rest[2 * n_tables + 2 :]
+    (
+        tau_ref, v_ref, links_ref, entry_ref, halo_x, field, turned, left, part, around_in, around, recv, total, half_in, window, far_in, every, local_sem, token, halo_send, halo_recv, around_send, around_recv, part_send, part_recv, half_send, half_recv, far_send, far_recv, last_send, last_recv,
+        table_sem, dirs_ref, moms_ref, pair_ref, small_sem,
+    ) = rest
     n_ta, n_gx, n_gy = sizes
     ta, gx, gy = (lax.axis_index(axis) for axis in ("ta", "gx", "gy"))
     cells_y = links_ref.shape[1]
@@ -87,49 +118,31 @@
             ((links_hbm, links_ref.at[core]), (v_hbm, v_ref.at[mine_at]), (perams_ref, tau_ref))
         )
     ]
-    for copy in locals_:
+    table_copies = [
+        pltpu.make_async_copy(src, dst, table_sem.at[i])
+        for i, (src, dst) in enumerate(zip(sources, tables))
+    ]
+    smalls = [
+        pltpu.make_async_copy(src, dst, small_sem.at[i])
+        for i, (src, dst) in enumerate(
+            ((dirs_hbm, dirs_ref), (moms_hbm, moms_ref), (pair_hbm, pair_ref))
+        )
+    ]
+    for copy in locals_[:2] + table_copies + smalls + locals_[2:]:
         copy.start()
-    n_k = entry_ref.shape[0]
-    row = iota((layer, layer), 0)
-    col = iota((layer, layer), 1)
-    same_site = row // 6 == col // 6
-    shift = ones_where(col == lax.rem(row + 6, layer)).astype(BF16)
-    shift_back = ones_where(row == lax.rem(col + 6, layer)).astype(BF16)
-    turn = (
-        ones_where((row % 2 == 1) & (col == row - 1)) - ones_where((row % 2 == 0) & (col == row + 1))
-    ).astype(BF16)
-    pick = ones_where(iota((layer, cells_z), 0) // 6 == iota((layer, cells_z), 1))
-    k_row = iota((layer, n_k), 0)
-    k_col = iota((layer, n_k), 1)
-    color_of_row = (k_row // 2) % 3
-    keep_row = color_of_row == (k_col // 6) % 3
-    keep_col = color_of_row == (k_col // 2) % 3
-    k = iota((n_k, layer), 0)
-    c = iota((n_k, layer), 1)
-    even = row % 2 == 0
-
-    z_coord = iota((cells_z, 128), 0).astype(F32)
-    for mom in range(3):
-        angle = (2.0 * math.pi * mom) * z_coord / cells_z
-        cos_ref[mom] = jnp.dot(pick, jnp.cos(angle), precision=lax.Precision.HIGHEST, preferred_element_type=F32)
-        sin_ref[mom] = jnp.dot(pick, jnp.sin(angle), precision=lax.Precision.HIGHEST, preferred_element_type=F32)
+    turn, shift, shift_back, same_site, pick_b, row_plain, row_turned, col_plain, unit, *maps = (
+        ref for ref in tables[: len(tables) - 2]
+    )
+    cos_ref, sin_ref = tables[-2:]
+    n_k = maps[0].shape[0] // 2
+    block = turn.shape[0]
 
     def put(code, at, plain, rotated):
-        field[code, at] = plain
-        turned[code, at] = rotated
-
-    maps = []
-    for d in range(3):
-        in_d = k // 18 == d
-        re_k, im_k = k % 2 == 0, k % 2 == 1
-        re_c, im_c = c % 2 == 0, c % 2 == 1
-        b_match = in_d & ((k // 2) % 3 == (c // 2) % 3)
-        a_match = in_d & ((k // 6) % 3 == (c // 2) % 3)
-        g_re = ones_where(b_match & re_c & re_k) - ones_where(b_match & im_c & im_k)
-        g_im = ones_where(b_match & re_c & im_k) + ones_where(b_match & im_c & re_k)
-        h_re = ones_where(a_match & re_c & re_k) + ones_where(a_match & im_c & im_k)
-        h_im = ones_where(a_match & im_c & re_k) - ones_where(a_match & re_c & im_k)
-        maps.append([m.astype(BF16) for m in (g_re, g_im, h_re, h_im)])
+        field[code, pl.ds(*at)] = plain
+        turned[code, pl.ds(*at)] = rotated
+
+    def part_of(x, i):
+        return x[i * block : (i + 1) * block]
 
     pl.semaphore_wait(barrier, len(known) + 2)
     halos = [
@@ -174,67 +187,82 @@
 
     tell("a")
 
-    pick_b = pick.astype(BF16)
     forward = []
     for own in (True, False):
         if own:
-            locals_[0].wait()
-            locals_[1].wait()
+            for copy in locals_[:2] + table_copies + smalls:
+                copy.wait()
         else:
             heard("a")
             tell("b")
             halos[1].wait_recv()
             halos[2].wait_recv()
         whose = core if own else 1 - core
+        base = pl.multiple_of(whose * rows, rows)
+        spots = [(pl.multiple_of(base + i * block, block), block) for i in range(rows // block)]
+        after = [(pl.multiple_of(base + layer + i * block, block), block) for i in range(rows // block)]
+        lists = []
         for y in range(cells_y):
-            at = pl.ds(pl.multiple_of(whose * rows + y * layer, layer), layer)
-            after = pl.ds(pl.multiple_of(whose * rows + (y + 1) * layer, layer), layer)
             for kk in range(links_ref.shape[2]):
-                entry_ref[pl.ds(2 * kk, 2), :] = links_ref[whose, y, kk].astype(F32)
-            v_y = v_ref[at, :]
-            put(6, at, v_y.astype(F32), mm(turn, v_y))
-            entries = mm_nt(pick_b, entry_ref[...].astype(BF16))
-            by_row = jnp.where(keep_row, entries, 0.0).astype(BF16)
-            by_col = jnp.where(keep_col, entries, 0.0).astype(BF16)
+                entry = links_ref[whose, y, kk].astype(F32)
+                entry_ref[2 * own + y, pl.ds(2 * kk, 2), :] = entry
+                entry_ref[2 * own + y, pl.ds(n_k + 2 * kk, 2), :] = entry
+            lists.append(mm_nt(pick_b[...], entry_ref[2 * own + y].astype(BF16)).astype(BF16))
+        by_row = jnp.concatenate([x * row_plain[...] for x in lists], axis=0)
+        by_row_turned = jnp.concatenate([x * row_turned[...] for x in lists], axis=0)
+        by_col = jnp.concatenate([x * col_plain[...] for x in lists], axis=0)
+        site = jnp.concatenate([same_site[...]] * cells_y, axis=0)
+        apply, apply_turned, adjoint = [], [], []
+        for d in range(3):
+            apply.append(mm(by_row, maps[2 * d][...]).astype(BF16) * site)
+            apply_turned.append(mm(by_row_turned, maps[2 * d][...]).astype(BF16) * site)
+            adjoint.append(mm(by_col, maps[2 * d + 1][...]).astype(BF16) * site)
+        v_own = v_ref[pl.ds(base, rows), :]
+        carried = [[], [], []]
+        for i, spot in enumerate(spots):
+            stack = jnp.concatenate([part_of(x, i) for x in adjoint] + [turn[...]], axis=0)
+            product = mm(stack, part_of(v_own, i))
+            put(6, spot, part_of(v_own, i).astype(F32), part_of(product, 3))
             for d in range(3):
-                g_re, g_im, h_re, h_im = maps[d]
-                q_re = mm(by_row, g_re)
-                q_im = mm(by_row, g_im)
-                apply = jnp.where(same_site, jnp.where(even, q_re, q_im), 0.0).astype(BF16)
-                apply_turned = jnp.where(same_site, jnp.where(even, -q_im, q_re), 0.0).astype(BF16)
-                p_re = mm(by_col, h_re)
-                p_im = mm(by_col, h_im)
-                adjoint = jnp.where(same_site, jnp.where(even, p_re, p_im), 0.0).astype(BF16)
-                carried = mm(adjoint, v_y).astype(BF16)
+                carried[d].append(part_of(product, d).astype(BF16))
+        per = layer // block
+        v_next, moved = [], []
+        for y in range(cells_y):
+            v_next.append(mm(shift[...], v_own[y * layer : (y + 1) * layer]).astype(BF16))
+            moved.append(mm(shift_back[...], jnp.concatenate(carried[2][y * per : (y + 1) * per], axis=0)).astype(BF16))
+        for i, spot in enumerate(spots):
+            back = [carried[0][i], carried[1][i], part_of(moved[i // per], i % per)]
+            back_turned = mm(turn[...], jnp.concatenate(back, axis=1))
+            lanes = back[0].shape[1]
+            for d in range(3):
+                put(3 + d, spot, back[d].astype(F32), back_turned[:, d * lanes : (d + 1) * lanes])
+                pair = jnp.concatenate([part_of(apply[d], i), part_of(apply_turned[d], i)], axis=0)
                 if d == 2:
-                    carried = mm(shift_back, carried).astype(BF16)
-                    v_next = mm(shift, v_y).astype(BF16)
-                    put(2, at, mm(apply, v_next), mm(apply_turned, v_next))
+                    product = mm(pair, part_of(v_next[i // per], i % per))
+                    put(2, spot, product[:block], product[block:])
                 else:
-                    forward.append((d, at, after, apply, apply_turned))
-                put(3 + d, at, carried.astype(F32), mm(turn, carried))
+                    forward.append((d, spot, after[i], pair))
 
     vectors = v_ref.shape[1]
-    unit = ones_where(iota((vectors, vectors), 0) == iota((vectors, vectors), 1)).astype(BF16)
-    left[0] = mm_nt(unit, v_ref[pl.ds(0, 2 * rows), :]).astype(BF16)
+    left[0] = mm_nt(unit[...], v_ref[pl.ds(0, 2 * rows), :]).astype(BF16)
 
     edges[0].wait_recv()
-    left[2] = mm_nt(unit, v_ref[pl.ds(layer, 2 * rows), :]).astype(BF16)
-    for d, at, after, apply, apply_turned in forward:
+    left[2] = mm_nt(unit[...], v_ref[pl.ds(layer, 2 * rows), :]).astype(BF16)
+    for d, at, after, pair in forward:
         if d == 1:
-            v_next = v_ref[after, :]
-            put(1, at, mm(apply, v_next), mm(apply_turned, v_next))
+            product = mm(pair, v_ref[pl.ds(*after), :])
+            put(1, at, product[:block], product[block:])
     halos[0].wait_recv()
     halos[3].wait_recv()
     heard("b")
     if far:
         tell("c")
     tell("e")
-    left[1] = mm_nt(unit, halo_x[...]).astype(BF16)
-    for d, at, after, apply, apply_turned in forward:
+    left[1] = mm_nt(unit[...], halo_x[...]).astype(BF16)
+    for d, at, after, pair in forward:
         if d == 0:
-            v_next = halo_x[at, :]
-            put(0, at, mm(apply, v_next), mm(apply_turned, v_next))
+            product = mm(pair, halo_x[pl.ds(*at), :])
+            put(0, at, product[:block], product[block:])
     chunk = vectors // 4
     n_y = n_gy // 2
     row_y = gy // 2
@@ -370,8 +398,9 @@
             y_im = y_block[s * vectors : (s + 1) * vectors, vectors:]
             sum_re = sum_re + (x_re * y_re + x_im * y_im)
             sum_im = sum_im + (x_im * y_re - x_re * y_im)
-    corr_ref[0, 0] = jnp.sum(sum_re) / vectors
-    corr_ref[0, 1] = jnp.sum(sum_im) / vectors
+    traces = [jnp.sum(jnp.sum(x, axis=0, keepdims=True), axis=1, keepdims=True) for x in (sum_re, sum_im)]
+    part_at = lax.broadcasted_iota(jnp.int32, (1, 2), 1)
+    corr_ref[...] = jnp.where(part_at == 0, *traces) / vectors
 
     for copy in [*halos, *arounds, *sends.values(), *halves, *fars, *lasts]:
         copy.wait_send()
@@ -398,30 +427,29 @@
         chunk = vectors // 4
         piece = (chunk, 2 * vectors)
         half = (chunk // 2, 2 * vectors)
-        smem = pl.BlockSpec(memory_space=pltpu.SMEM)
+        tables = [jnp.asarray(t, BF16) for t in selections(cells_z, vectors)] + [jnp.asarray(t, F32) for t in phases(cells_z, vectors)]
         vmem = pl.BlockSpec(memory_space=pltpu.VMEM)
         hbm = pl.BlockSpec(memory_space=pltpu.HBM)
         dma = pltpu.SemaphoreType.DMA
         margins, corr = pl.pallas_call(
-            lambda *refs: kernel(sizes, cells_z, norm_factor, *refs),
+            lambda *refs: kernel(sizes, len(tables), norm_factor, *refs),
             name="meson_step",
             out_shape=(
                 pltpu.VMEM((2, vectors, vectors), BF16),
-                jax.ShapeDtypeStruct((1, 2), F32),
+                pltpu.VMEM((1, 2), F32),
             ),
-            in_specs=[smem, smem, smem, hbm, hbm, hbm],
-            out_specs=(vmem, smem),
+            in_specs=[hbm] * (6 + len(tables)),
+            out_specs=(vmem, vmem),
             scratch_shapes=[
+                *(pltpu.VMEM(table.shape, table.dtype) for table in tables),
                 pltpu.VMEM((2, order, order), BF16),
                 pltpu.VMEM((2 * rows + layer, vectors), BF16),
                 pltpu.VMEM((2, cells_y, n_k // 2, 2, cells_z), BF16),
-                pltpu.VMEM((n_k, cells_z), F32),
+                pltpu.VMEM((2 * cells_y, 2 * n_k, cells_z), F32),
                 pltpu.VMEM((2 * rows, vectors), BF16),
                 pltpu.VMEM((7, 2 * rows, vectors), F32),
                 pltpu.VMEM((7, 2 * rows, vectors), F32),
                 pltpu.VMEM((3, vectors, 2 * rows), BF16),
-                pltpu.VMEM((3, layer, vectors), F32),
-                pltpu.VMEM((3, layer, vectors), F32),
                 pltpu.VMEM((4, 4, *piece), F32),
                 pltpu.VMEM((4, *piece), F32),
                 pltpu.VMEM((4, *piece), F32),
@@ -445,9 +473,14 @@
                 dma((n_far,)),
                 dma((sizes[0] * 8,)),
                 dma((sizes[0] * 8,)),
+                dma((len(tables),)),
+                pltpu.SMEM(op_dirs.shape, jnp.int32),
+                pltpu.SMEM(op_moms.shape, jnp.int32),
+                pltpu.SMEM(pair_times.shape, jnp.int32),
+                dma((3,)),
             ],
             compiler_params=pltpu.CompilerParams(collective_id=0, has_side_effects=True, vmem_limit_bytes=56000 * 1024),
-        )(op_dirs, op_moms, pair_times, field, link_rows, perams[0])
+        )(op_dirs, op_moms, pair_times, field, link_rows, perams[0], *tables)
         return margins.astype(F32)[None, None], corr[None]
 
     placed = (

time: 63.9 us -> 61.8 us (0.967)
  Pallas kernels: 62 us -> 59.8 us
    pallas_call x1, Pallas kernels: 62 us -> 59.8 us  [per_device(): pl.pallas_call(lambda *refs: kernel(sizes, len(tables), norm_factor, *ref...]
where the time goes in v4:
time: 61.8 us; the launch traced here: 61.6 us
  Pallas kernels  59.8 us (97%)
  other arithmetic  0.66 us (1%)
  between operations  0.64 us (1%)
    pallas_call x1, Pallas kernels, per_device(): pl.pallas_call(lambda *refs: kernel(sizes, len(tables), norm_factor, *ref...  59.8 us

profile of v4, /device:TPU:24, one launch (start us, length us, event | category | flops | bytes accessed | tf_op | source)
XLA Modules:
  0.0 61.6 jit_solution(9184746281799406659)
XLA Ops:
  0.6 59.8 %meson_step.1 = (bf16[2,128,128]{2,1,0:T(8,128)(2,1)S(1)}, f32[1,2]{1,0:T(1,128)S(1)}) custom-call(s32[8]{0:T(128)} %refs_0_.1, s32[8]{0:T(128)} %refs_1_.1, s32[1,2]{1,0:T(1,128)} %refs_2_.1, bf16[288,128]{1,0:T(8,128)(2,1)} %bitcast.13, bf16[2,27,2,24]{3,2,1,0:T(2,128)(2,1)} %bitcast.14, bf16[2,512,512]{2,1,0:T(8,128)(2,1)} %bitcast.12, ...), custom_call_target="tpu_custom_call" | custom-call | tf_op jit(solution)/shard_map/meson_step/pallas_call | solution.py:434
  60.5 0.5 copy.26
  61.0 0.7 %bitcast_convert_fusion = f32[1,1,2,128,128]{4,3,2,1,0:T(8,128)} fusion(bf16[2,128,128]{2,1,0:T(8,128)(2,1)S(1)} %get-tuple-element.4), kind=kLoop, calls=%fused_computation | loop fusion | flops 32768 | bytes 196608 | tf_op jit(solution)/shard_map/broadcast_in_dim | solution.py:484

commit v5 on v4

--- a/solution.py
+++ b/solution.py
@@ -145,12 +145,17 @@
         return x[i * block : (i + 1) * block]
 
     pl.semaphore_wait(barrier, len(known) + 2)
+    low = pl.ds(pl.multiple_of(core * rows, layer), layer)
+    high = pl.ds(pl.multiple_of(core * rows + layer, layer), rows - layer)
+    v_high = v_hbm.at[pl.ds(layer, rows - layer)]
     halos = [
-        remote(v_hbm, halo_x.at[mine_at], halo_send.at[0], halo_recv.at[0], 0, -1, 0),
+        remote(v_hbm.at[pl.ds(0, layer)], halo_x.at[low], halo_send.at[0], halo_recv.at[0], 0, -1, 0),
         remote(v_hbm, v_ref.at[mine_at], halo_send.at[1], halo_recv.at[1], 0, 0, flip),
         remote(links_hbm, links_ref.at[core], halo_send.at[2], halo_recv.at[2], 0, 0, flip),
-        remote(v_hbm, halo_x.at[mine_at], halo_send.at[3], halo_recv.at[3], 0, -1, flip),
+        remote(v_high, halo_x.at[high], halo_send.at[3], halo_recv.at[3], 0, -1, flip),
+        remote(v_high, halo_x.at[high], halo_send.at[6], halo_recv.at[5], 0, -1, 0),
     ]
+    passed = remote(halo_x.at[low], halo_x.at[low], halo_send.at[7], halo_recv.at[6], 0, 0, flip)
     edge = v_hbm.at[pl.ds(0, layer)]
     edge_to = v_ref.at[pl.ds(2 * rows, layer)]
     edges = [
@@ -195,6 +200,8 @@
         else:
             heard("a")
             tell("b")
+            halos[0].wait_recv()
+            passed.start()
             halos[1].wait_recv()
             halos[2].wait_recv()
         whose = core if own else 1 - core
@@ -252,8 +259,8 @@
         if d == 1:
             product = mm(pair, v_ref[pl.ds(*after), :])
             put(1, at, product[:block], product[block:])
-    halos[0].wait_recv()
-    halos[3].wait_recv()
+    for copy in (passed, *halos[3:]):
+        copy.wait_recv()
     heard("b")
     if far:
         tell("c")
@@ -402,7 +409,7 @@
     part_at = lax.broadcasted_iota(jnp.int32, (1, 2), 1)
     corr_ref[...] = jnp.where(part_at == 0, *traces) / vectors
 
-    for copy in [*halos, *arounds, *sends.values(), *halves, *fars, *lasts]:
+    for copy in [*halos, passed, *arounds, *sends.values(), *halves, *fars, *lasts]:
         copy.wait_send()
 
     @pl.when(core == 0)
@@ -461,8 +468,8 @@
                 pltpu.VMEM((sizes[0], 8, *half), BF16),
                 dma((3,)),
                 pltpu.SemaphoreType.REGULAR((12,)),
-                dma((6,)),
-                dma((5,)),
+                dma((8,)),
+                dma((7,)),
                 dma((4,)),
                 dma((4,)),
                 dma((12,)),

time: 61.8 us -> 61.2 us (level)
  no operation moved by 1% of the time
where the time goes in v5:
time: 61.2 us; the launch traced here: 61 us
  Pallas kernels  59.2 us (97%)
  other arithmetic  0.66 us (1%)
  between operations  0.64 us (1%)
    pallas_call x1, Pallas kernels, per_device(): pl.pallas_call(lambda *refs: kernel(sizes, len(tables), norm_factor, *ref...  59.2 us

profile of v5, /device:TPU:24, one launch (start us, length us, event | category | flops | bytes accessed | tf_op | source)
XLA Modules:
  0.0 61.0 jit_solution(14382357732421165803)
XLA Ops:
  0.6 59.2 %meson_step.1 = (bf16[2,128,128]{2,1,0:T(8,128)(2,1)S(1)}, f32[1,2]{1,0:T(1,128)S(1)}) custom-call(s32[8]{0:T(128)} %refs_0_.1, s32[8]{0:T(128)} %refs_1_.1, s32[1,2]{1,0:T(1,128)} %refs_2_.1, bf16[288,128]{1,0:T(8,128)(2,1)} %bitcast.13, bf16[2,27,2,24]{3,2,1,0:T(2,128)(2,1)} %bitcast.14, bf16[2,512,512]{2,1,0:T(8,128)(2,1)} %bitcast.12, ...), custom_call_target="tpu_custom_call" | custom-call | tf_op jit(solution)/shard_map/meson_step/pallas_call | solution.py:441
  59.9 0.5 copy.26
  60.4 0.7 %bitcast_convert_fusion = f32[1,1,2,128,128]{4,3,2,1,0:T(8,128)} fusion(bf16[2,128,128]{2,1,0:T(8,128)(2,1)S(1)} %get-tuple-element.4), kind=kLoop, calls=%fused_computation | loop fusion | flops 32768 | bytes 196608 | tf_op jit(solution)/shard_map/broadcast_in_dim | solution.py:491
